TPU v7x, 768 devices: a whole 4x8x12 slice. The times are simulated.
768 devices in a mesh: seq: 32 (over z_hi, y), chan: 24 (over z_lo, x, core).
Axes of the slice: x: 4, y: 8, z: 12 (z_hi: 4, z_lo: 3; z = z_hi * 3 + z_lo), core: 2. Of those that a mesh axis runs over, the one named last changes fastest.
Arguments:
- query_in: bfloat16 [4096, 6144], P('seq', 'chan'), may hold values from -6 to 6
- key_in: bfloat16 [4096, 6144], P('seq', 'chan'), may hold values from -6 to 6
- value_in: bfloat16 [4096, 6144], P('seq', 'chan'), may hold values from -6 to 6
- filters: bfloat16 [384, 128], P('chan'), may hold values from -0.5 to 0.5
- doc_lengths: int32 [16], replicated, may hold values from 1 to 1024, 4096 in all
- w_out: bfloat16 [6144, 6144], P('chan'), may hold values from -0.125 to 0.125
- cotangent: bfloat16 [4096, 6144], P('seq', 'chan'), may hold values from -6 to 6
Outputs:
- block_out: bfloat16 [4096, 6144], P('seq', 'chan')
- grad_query: bfloat16 [4096, 6144], P('seq', 'chan')
- grad_key: bfloat16 [4096, 6144], P('seq', 'chan')
- grad_value: bfloat16 [4096, 6144], P('seq', 'chan')
- grad_w_out: bfloat16 [6144, 6144], P('chan', 'seq')
- grad_filters: float32 [384, 128], P('chan', 'seq')
Inputs may be any that keep to these rules, and one draw needn't show every extreme that they name: `doc_lengths`: the lengths sum to 4096.
All inputs are finite; a program needn't handle non-finite values.
Results may differ from a plain program's by a relative error of at most 0.02.
Values may be sent and summed in bfloat16 or wider, within the bound.
No kernel may reach another device: no remote copies, remote signals or barrier semaphores. Data moves between devices by JAX's collectives and lax.ppermute only.
A program may use at most 32 MiB of HBM per device.

v0:
```python
import jax
import jax.numpy as jnp
from jax import lax
from jax.sharding import PartitionSpec as P


def from_behind(value, axis, steps):
    count = lax.axis_size(axis)
    leading, last = (max(0, -steps), min(count, count - steps))
    return lax.ppermute(value, axis, [(source, source + steps) for source in range(leading, last)])


def doc_start(positions, starts):
    before = starts[None, :] <= positions[:, None]
    return jnp.max(jnp.where(before, starts[None, :], 0), axis=1)


def banded(tap_rows, tok_rows):
    group_count, length = tap_rows.shape
    padded = jnp.concatenate([tap_rows, jnp.zeros((group_count, tok_rows), tap_rows.dtype)], axis=1)
    tiled_taps = jnp.tile(padded, (1, tok_rows))
    return tiled_taps[:, : tok_rows * (tok_rows + length - 1)].reshape(
        group_count, tok_rows, tok_rows + length - 1
    )


def collect(cotangent, w_out, gated):
    shard_piece = lax.all_gather(cotangent, "chan", axis=1, tiled=True)
    grad_in = jnp.einsum("tn,cn->tc", shard_piece, w_out, preferred_element_type=jnp.float32)
    weight_block = jnp.einsum("tc,tn->cn", gated, shard_piece, preferred_element_type=jnp.float32)
    return (grad_in, weight_block)


def apply_filter(forward_band, mixed_ext, query_in):
    tok_rows, chan_count = query_in.shape
    group_count = forward_band.shape[0]
    grouped = mixed_ext.reshape(mixed_ext.shape[0], group_count, chan_count // group_count)
    filtered = jnp.einsum(
        "gti,igc->tgc", forward_band, grouped, preferred_element_type=jnp.float32
    ).reshape(tok_rows, chan_count)
    gated = (query_in.astype(jnp.float32) * filtered).astype(jnp.bfloat16)
    return (filtered, gated)


def project(gated, w_out):
    partial_out = jnp.dot(gated, w_out, preferred_element_type=jnp.float32)
    return lax.psum_scatter(
        partial_out.astype(jnp.bfloat16), "chan", scatter_dimension=1, tiled=True
    )


def body(query_in, key_in, value_in, filters, doc_lengths, w_out, cotangent):
    tok_rows, chan_count = query_in.shape
    group_count, length = filters.shape
    tap_reach = length - 1
    product_kv = (key_in.astype(jnp.float32) * value_in.astype(jnp.float32)).astype(jnp.bfloat16)
    starts = jnp.cumsum(doc_lengths) - doc_lengths
    first_row = lax.axis_index("seq") * tok_rows
    local_steps = jnp.arange(tok_rows, dtype=jnp.int32)
    wide_steps = jnp.arange(tok_rows + tap_reach, dtype=jnp.int32)
    own_pos = first_row + local_steps
    fwd_mask = (first_row - tap_reach + wide_steps)[None, :] >= doc_start(own_pos, starts)[:, None]
    back_mask = own_pos[:, None] >= doc_start(first_row + wide_steps, starts)[None, :]
    forward_band = banded(jnp.flip(filters, 1), tok_rows) * fwd_mask.astype(jnp.bfloat16)[None]
    backward_band = banded(filters, tok_rows) * back_mask.astype(jnp.bfloat16)[None]
    earlier = from_behind(product_kv[tok_rows - tap_reach :], "seq", 1)
    mixed_ext = jnp.concatenate([earlier, product_kv], axis=0)
    filtered, gated = apply_filter(forward_band, mixed_ext, query_in)
    block_out = project(gated, w_out)
    grad_in, weight_part = collect(cotangent, w_out, gated)
    grad_gate = (grad_in * query_in.astype(jnp.float32)).astype(jnp.bfloat16)
    later_rows = from_behind(grad_gate[:tap_reach], "seq", -1)
    grad_ext = jnp.concatenate([grad_gate, later_rows], axis=0)
    grad_query = (grad_in * filtered).astype(jnp.bfloat16)
    per_group = chan_count // group_count
    grad_mixed = jnp.einsum(
        "gtr,rgc->tgc",
        backward_band,
        grad_ext.reshape(tok_rows + tap_reach, group_count, per_group),
        preferred_element_type=jnp.float32,
    ).reshape(tok_rows, chan_count)
    grad_key = (grad_mixed * value_in.astype(jnp.float32)).astype(jnp.bfloat16)
    grad_value = (grad_mixed * key_in.astype(jnp.float32)).astype(jnp.bfloat16)
    pair_terms = jnp.einsum(
        "tgc,igc->gti",
        grad_gate.reshape(tok_rows, group_count, per_group),
        mixed_ext.reshape(tok_rows + tap_reach, group_count, per_group),
        preferred_element_type=jnp.float32,
    )
    pair_terms = pair_terms * fwd_mask.astype(jnp.float32)[None]
    flat_pairs = pair_terms.reshape(group_count, tok_rows * (tok_rows + tap_reach))
    flat_pairs = jnp.concatenate(
        [flat_pairs, jnp.zeros((group_count, tok_rows), jnp.float32)], axis=1
    )
    diagonals = flat_pairs.reshape(group_count, tok_rows, tok_rows + length)[:, :, :length]
    tap_part = jnp.flip(jnp.sum(diagonals, axis=1), 1)
    weight_sum, tap_sum = (
        lax.psum_scatter(
            weight_part.astype(jnp.bfloat16), "seq", scatter_dimension=1, tiled=True
        ).astype(jnp.float32),
        lax.psum_scatter(
            tap_part.astype(jnp.bfloat16), "seq", scatter_dimension=1, tiled=True
        ).astype(jnp.float32),
    )
    return (block_out, grad_query, grad_key, grad_value, weight_sum.astype(jnp.bfloat16), tap_sum)


def solution(mesh):
    return jax.shard_map(
        body,
        mesh=mesh,
        in_specs=(
            P("seq", "chan"),
            P("seq", "chan"),
            P("seq", "chan"),
            P("chan", None),
            P(),
            P("chan", None),
            P("seq", "chan"),
        ),
        out_specs=(
            P("seq", "chan"),
            P("seq", "chan"),
            P("seq", "chan"),
            P("seq", "chan"),
            P("chan", "seq"),
            P("chan", "seq"),
        ),
        check_vma=False,
    )
```

profile of v0, /device:TPU:6, one launch (start us, length us, event | category | flops | bytes accessed | tf_op | source)
XLA Modules:
  0.0 522.7 jit_solution(9734036252779678896)
XLA Ops:
  7.2 0.7 all-gather.2.cloned.1.call-update
  7.9 0.0 reduce-scatter.3.cloned.1.call-start
  8.0 0.9 copy.39
  8.9 0.1 reduce
  9.0 0.7 sub.7
  9.7 0.7 concatenate.18
  10.4 0.1 tile.20
  10.4 0.6 copy.48
  11.0 1.1 slice.23
  12.1 5.6 %reshape.173 = bf16[16,128,255]{2,1,0:T(8,128)(2,1)} reshape(bf16[16,32640]{1,0:T(8,128)(2,1)} %slice.23) | data formatting | bytes 2088960 | tf_op jit(solution)/shard_map/reshape | solution.py:22
  17.8 0.1 select_reduce_fusion.1
  17.9 0.1 select_reduce_fusion
  17.9 0.7 compare_convert_fusion.2
  18.7 76.5 %all-gather.2.cloned.1.call-done = bf16[128,6144]{1,0:T(8,128)(2,1)} async-done(((bf16[128,256]{1,0:T(8,128)(2,1)}), bf16[128,6144]{1,0:T(8,128)(2,1)}) %all-gather.2.cloned.1.call-update) | async-done | bytes 1572880 | tf_op jit(solution)/shard_map/all_gather | solution.py:28
  95.2 3.2 fusion.7
  98.5 1.4 collective-permute-start.1
  99.9 4.9 collective-permute-done.1
  104.8 0.1 copy.42
  104.9 2.3 fusion
  107.2 1.0 copy.43
  108.2 1.6 fusion.8
  109.8 3.4 collective-permute-start
  113.2 0.7 compare_convert_fusion
  113.9 0.1 rev.8
  114.0 0.1 tile.8
  114.1 0.6 copy.47
  114.7 1.1 slice.21
  115.8 5.6 %reshape.168 = bf16[16,128,255]{2,1,0:T(8,128)(2,1)} reshape(bf16[16,32640]{1,0:T(8,128)(2,1)} %slice.21) | data formatting | bytes 2088960 | tf_op jit(solution)/shard_map/reshape | solution.py:22
  121.4 0.7 pad_maximum_fusion
  122.1 1.0 copy.38
  123.1 2.3 fusion.2
  125.4 1.0 copy.40
  126.4 1.8 convolution_convert_fusion.1
  128.2 0.2 reduce-scatter.5.cloned.1.call-start
  128.4 4.1 convolution_convert_fusion
  132.6 1.3 dynamic-slice
  134.5 0.1 copy.45
  134.6 2.8 convolution_multiply_fusion
  137.4 4.1 reshape.176
  141.5 1.7 concatenate.19
  143.2 0.6 copy.49
  143.8 0.1 slice_reduce_fusion
  143.9 0.1 rev.9
  144.0 0.1 copy.46
  144.2 170.3 %all-reduce.3 = bf16[16,128]{0,1:T(8,128)(2,1)S(1)} all-reduce(bf16[16,128]{0,1:T(8,128)(2,1)S(1)} %copy.46), channel_id=4, replica_groups=mesh['seq'=32,'chan'=24] {'seq'}, use_global_device_ids=true, to_apply=%region_6.7.clone | all-reduce | flops 2048 | bytes 8192
  314.5 0.6 dynamic-slice_convert_fusion
  315.1 0.6 multiply_convert_fusion
  315.7 200.5 %reduce-scatter.5.cloned.1.call-done = bf16[256,192]{0,1:T(8,128)(2,1)} async-done(((bf16[256,6144]{0,1:T(8,128)(2,1)}), bf16[256,192]{0,1:T(8,128)(2,1)}) %reduce-scatter.5.cloned.1.call-update) | async-done | bytes 98320 | tf_op jit(solution)/shard_map/reduce_scatter | solution.py:98
  (20 shorter events, 0.2 us)
Async XLA Ops:
  7.2 88.0 %copy-start = (bf16[256,6144]{1,0:T(8,128)(2,1)S(1)}, bf16[256,6144]{1,0:T(8,128)(2,1)}, u32[]{:S(2)}) copy-start(bf16[256,6144]{1,0:T(8,128)(2,1)} %param.12) | copy-start | bytes 9437188
  7.2 88.0 %all-gather.2.cloned.1.call-start = ((), (), s32[]{:S(2)}) async-start(), calls=%async_computation.3 | async-start | bytes 1638400 | tf_op jit(solution)/shard_map/all_gather | solution.py:28
  7.9 307.8 %reduce-scatter.3.cloned.1.call-start = ((), (), s32[]{:S(2)}) async-start(), calls=%async_computation.2 | async-start | bytes 1638400 | tf_op jit(solution)/shard_map/reduce_scatter | solution.py:47
  11.0 84.2 %copy-start.1 = (bf16[128,256]{1,0:T(8,128)(2,1)S(1)}, bf16[128,256]{1,0:T(8,128)(2,1)}, u32[]{:S(2)}) copy-start(bf16[128,256]{1,0:T(8,128)(2,1)} %param.7) | copy-start | bytes 196612
  98.4 15.5 %copy-start.3 = (bf16[16,128]{1,0:T(8,128)(2,1)S(1)}, bf16[16,128]{1,0:T(8,128)(2,1)}, u32[]{:S(2)}) copy-start(bf16[16,128]{1,0:T(8,128)(2,1)} %param.10) | copy-start | bytes 12292
  98.5 6.4 %collective-permute-start.1 = (bf16[127,256]{1,0:T(8,128)(2,1)S(1)}, bf16[127,256]{1,0:T(8,128)(2,1)S(1)}, u32[]{:S(2)}, u32[]{:S(2)}) collective-permute-start(bf16[127,256]{1,0:T(8,128)(2,1)S(1)} %bitcast.34), channel_id=1, source_target_pairs={{24,0},{48,24},{72,48},{96,72},{120,96},{144,120},{168,144},{192,1... | collective-permute-start | bytes 195080 | tf_op jit(solution)/shard_map/ppermute | solution.py:10
  109.8 11.6 %collective-permute-start = (bf16[127,256]{1,0:T(8,128)(2,1)S(1)}, bf16[127,256]{1,0:T(8,128)(2,1)S(1)}, u32[]{:S(2)}, u32[]{:S(2)}) collective-permute-start(bf16[127,256]{1,0:T(8,128)(2,1)S(1)} %slice.20), channel_id=1, source_target_pairs={{0,24},{24,48},{48,72},{72,96},{96,120},{120,144},{144,168},{168,1... | collective-permute-start | bytes 195080 | tf_op jit(solution)/shard_map/ppermute | solution.py:10
  128.2 387.9 %reduce-scatter.5.cloned.1.call-start = ((), (), s32[]{:S(2)}) async-start(), calls=%async_computation.4 | async-start | bytes 3244032 | tf_op jit(solution)/shard_map/reduce_scatter | solution.py:98
  143.2 171.8 %copy-start.2 = (f32[128,256]{1,0:T(8,128)S(1)}, f32[128,256]{1,0:T(8,128)}, u32[]{:S(2)}) copy-start(f32[128,256]{1,0:T(8,128)} %get-tuple-element.12) | copy-start | bytes 393220
Sparse Core Ops, SparseCore 0:
  10.3 84.8 all-gather.1
  128.3 112.1 reduce-scatter.2
  246.2 269.9 reduce-scatter.4
where the time goes:
time: 523 us
  waiting for transfers between devices  283 us (54%)
  blocking collectives  170 us (33%)
  local copies, waits for them, and re-layouts  27.6 us (5%)
  matrix products  16.5 us (3%)
  between operations  14.5 us (3%)
  other arithmetic  6 us (1%)
    reduce_scatter x1, waiting for transfers between devices, body(): lax.psum_scatter(weight_part.astype(jnp.bfloat16), 'seq', scatter_dimensi...  200 us
    unnamed x1, blocking collectives  170 us
    all_gather x1, waiting for transfers between devices, collect(): shard_piece = lax.all_gather(cotangent, 'chan', axis=1, tiled=True)  76.5 us
    reshape x2, local copies, waits for them, and re-layouts, banded(): tiled_taps[:, :tok_rows * (tok_rows + length - 1)]  11.2 us
  transfers between devices with their start and end apart: 5, of which 3 were waited for; matrix products, arithmetic and copies ran while one was open for 7% of the time, Pallas kernels for 0%

commit v1 on v0

v1 whole, which is shorter than its diff:
```python
import jax
import jax.numpy as jnp
from jax import lax
from jax.sharding import Mesh, PartitionSpec as P

SEQ, CHAN = ("zh", "y"), ("zl", "x", "core")


def from_behind(value, axis, steps):
    count = lax.axis_size(axis)
    leading, last = (max(0, -steps), min(count, count - steps))
    return lax.ppermute(value, axis, [(source, source + steps) for source in range(leading, last)])


def doc_start(positions, starts):
    before = starts[None, :] <= positions[:, None]
    return jnp.max(jnp.where(before, starts[None, :], 0), axis=1)


def banded(tap_rows, tok_rows):
    group_count, length = tap_rows.shape
    padded = jnp.concatenate([tap_rows, jnp.zeros((group_count, tok_rows), tap_rows.dtype)], axis=1)
    tiled_taps = jnp.tile(padded, (1, tok_rows))
    return tiled_taps[:, : tok_rows * (tok_rows + length - 1)].reshape(
        group_count, tok_rows, tok_rows + length - 1
    )


def exchange(value, axes):
    return lax.all_to_all(value, axes, 0, 0, tiled=True)


def swap_cores(value):
    return lax.ppermute(value, "core", [(0, 1), (1, 0)])


def gather_rows(cotangent):
    tok_rows, width = cotangent.shape
    chips = lax.axis_size(("zl", "x"))
    mine = exchange(jnp.broadcast_to(cotangent[None], (chips, tok_rows, width)), ("zl", "x"))
    other = swap_cores(mine)
    first = lax.axis_index("core") == 0
    even, odd = jnp.where(first, mine, other), jnp.where(first, other, mine)
    pieces = [piece for pair in zip(even, odd) for piece in pair]
    return jnp.concatenate(pieces, axis=1)


def scatter_sum(partial):
    chips, cores, tok_rows, width = partial.shape
    core = lax.axis_index("core")
    kept = lax.dynamic_index_in_dim(partial, core, 1, keepdims=False)
    sent = lax.dynamic_index_in_dim(partial, 1 - core, 1, keepdims=False)
    pair = (kept + swap_cores(sent.astype(jnp.bfloat16)).astype(jnp.float32)).astype(jnp.bfloat16)
    return jnp.sum(exchange(pair, ("zl", "x")).astype(jnp.float32), axis=0)


def apply_filter(forward_band, mixed_ext, query_in):
    tok_rows, chan_count = query_in.shape
    group_count = forward_band.shape[0]
    grouped = mixed_ext.reshape(mixed_ext.shape[0], group_count, chan_count // group_count)
    filtered = jnp.einsum(
        "gti,igc->tgc", forward_band, grouped, preferred_element_type=jnp.float32
    ).reshape(tok_rows, chan_count)
    gated = (query_in.astype(jnp.float32) * filtered).astype(jnp.bfloat16)
    return (filtered, gated)


def body(query_in, key_in, value_in, filters, doc_lengths, w_out, cotangent):
    tok_rows, chan_count = query_in.shape
    group_count, length = filters.shape
    tap_reach = length - 1
    n_zh, n_y = lax.axis_size("zh"), lax.axis_size("y")
    n_chip = lax.axis_size(("zl", "x"))
    product_kv = (key_in.astype(jnp.float32) * value_in.astype(jnp.float32)).astype(jnp.bfloat16)
    earlier = from_behind(product_kv[tok_rows - tap_reach :], SEQ, 1)
    starts = jnp.cumsum(doc_lengths) - doc_lengths
    first_row = lax.axis_index(SEQ) * tok_rows
    local_steps = jnp.arange(tok_rows, dtype=jnp.int32)
    wide_steps = jnp.arange(tok_rows + tap_reach, dtype=jnp.int32)
    own_pos = first_row + local_steps
    fwd_mask = (first_row - tap_reach + wide_steps)[None, :] >= doc_start(own_pos, starts)[:, None]
    back_mask = own_pos[:, None] >= doc_start(first_row + wide_steps, starts)[None, :]
    forward_band = banded(jnp.flip(filters, 1), tok_rows) * fwd_mask.astype(jnp.bfloat16)[None]
    backward_band = banded(filters, tok_rows) * back_mask.astype(jnp.bfloat16)[None]
    rows = gather_rows(cotangent)
    grad_in = jnp.einsum("tn,cn->tc", rows, w_out, preferred_element_type=jnp.float32)
    grad_gate = (grad_in * query_in.astype(jnp.float32)).astype(jnp.bfloat16)
    later_rows = from_behind(grad_gate[:tap_reach], SEQ, -1)
    mixed_ext = jnp.concatenate([earlier, product_kv], axis=0)
    filtered, gated = apply_filter(forward_band, mixed_ext, query_in)
    grad_query = (grad_in * filtered).astype(jnp.bfloat16)
    w_parts = w_out.reshape(chan_count, n_chip, 2, chan_count)
    partial_out = jnp.einsum("tc,cjkn->jktn", gated, w_parts, preferred_element_type=jnp.float32)
    block_out = scatter_sum(partial_out).astype(jnp.bfloat16)
    grad_ext = jnp.concatenate([grad_gate, later_rows], axis=0)
    per_group = chan_count // group_count
    grad_mixed = jnp.einsum(
        "gtr,rgc->tgc",
        backward_band,
        grad_ext.reshape(tok_rows + tap_reach, group_count, per_group),
        preferred_element_type=jnp.float32,
    ).reshape(tok_rows, chan_count)
    grad_key = (grad_mixed * value_in.astype(jnp.float32)).astype(jnp.bfloat16)
    grad_value = (grad_mixed * key_in.astype(jnp.float32)).astype(jnp.bfloat16)
    pair_terms = jnp.einsum(
        "tgc,igc->gti",
        grad_gate.reshape(tok_rows, group_count, per_group),
        mixed_ext.reshape(tok_rows + tap_reach, group_count, per_group),
        preferred_element_type=jnp.float32,
    )
    pair_terms = pair_terms * fwd_mask.astype(jnp.float32)[None]
    flat_pairs = pair_terms.reshape(group_count, tok_rows * (tok_rows + tap_reach))
    flat_pairs = jnp.concatenate(
        [flat_pairs, jnp.zeros((group_count, tok_rows), jnp.float32)], axis=1
    )
    diagonals = flat_pairs.reshape(group_count, tok_rows, tok_rows + length)[:, :, :length]
    tap_part = jnp.flip(jnp.sum(diagonals, axis=1), 1).astype(jnp.bfloat16)
    owned = length // (n_zh * n_y)
    tap_rows = jnp.transpose(tap_part.reshape(group_count, n_zh, n_y, owned), (2, 1, 0, 3))
    tap_rows = tap_rows.reshape(n_y, n_zh, 1, group_count * owned)
    tap_rows = jnp.pad(tap_rows, ((0, 0), (0, 0), (0, 15), (0, chan_count - group_count * owned)))
    weight_part = jnp.einsum("tn,tc->nc", rows, gated, preferred_element_type=jnp.float32)
    weight_part = weight_part.astype(jnp.bfloat16)
    columns = weight_part.shape[0] // (n_zh * n_y)
    weight_part = jnp.transpose(weight_part.reshape(n_zh, n_y, columns, chan_count), (1, 0, 2, 3))
    terms = jnp.concatenate([weight_part, tap_rows], axis=2)
    over_y = jnp.sum(exchange(terms, "y").reshape(terms.shape).astype(jnp.float32), axis=0)
    over_seq = exchange(over_y.astype(jnp.bfloat16), "zh").astype(jnp.float32)
    total = jnp.sum(over_seq, axis=0)
    weight_sum = total[:columns].T.astype(jnp.bfloat16)
    tap_sum = total[columns, : group_count * owned].reshape(group_count, owned)
    return (block_out, grad_query, grad_key, grad_value, weight_sum, tap_sum)


def build(fine):
    both, rows = P(SEQ, CHAN), P(CHAN, None)
    return jax.shard_map(
        body,
        mesh=fine,
        in_specs=(both, both, both, rows, P(), rows, both),
        out_specs=(both, both, both, both, P(CHAN, SEQ), P(CHAN, SEQ)),
        check_vma=False,
    )


def solution(mesh):
    return build(Mesh(mesh.devices.reshape(4, 8, 3, 4, 2), SEQ + CHAN))
```

time: 523 us -> 217 us (0.41)
  waiting for transfers between devices: 283 us -> 94.7 us
  blocking collectives: 170 us -> 23.1 us
  starting transfers between devices: 5.1 us -> 41.9 us
  between operations: 14.5 us -> 1.18 us
  matrix products: 16.5 us -> 8.09 us
  other arithmetic: 6 us -> 12.8 us
  local copies, waits for them, and re-layouts: 27.6 us -> 34.2 us
    reduce_scatter x2 -> x0, waiting for transfers between devices: 200 us -> none  [the longest x1 200 us: body(): lax.psum_scatter(weight_part.astype(jnp.bfloat16), 'seq', scatter_dimensi...]
    unnamed x1 -> x0, blocking collectives: 170 us -> none
    all_to_all x0 -> x3, waiting for transfers between devices: none -> 87 us  [exchange(): return lax.all_to_all(value, axes, 0, 0, tiled=True)]
    all_gather x1 -> x0, waiting for transfers between devices: 76.5 us -> none  [collect(): shard_piece = lax.all_gather(cotangent, 'chan', axis=1, tiled=True)]
    all_to_all x0 -> x3, starting transfers between devices: none -> 33.1 us  [exchange(): return lax.all_to_all(value, axes, 0, 0, tiled=True)]
    all_to_all x0 -> x1, blocking collectives: none -> 23.1 us  [exchange(): return lax.all_to_all(value, axes, 0, 0, tiled=True)]
    reshape x0 -> x2, local copies, waits for them, and re-layouts: none -> 8.26 us  [the longest x1 8.06 us: body(): w_parts = w_out.reshape(chan_count, n_chip, 2, chan_count)]
  transfers between devices with their start and end apart: 5 -> 7, of which waited for: 3 -> 5; matrix products, arithmetic and copies ran while one was open for 7% -> 15% of each run, Pallas kernels for 0% -> 0%
where the time goes in v1:
time: 217 us; the launch traced here: 216 us
  waiting for transfers between devices  94.7 us (44%)
  starting transfers between devices  41.9 us (19%)
  local copies, waits for them, and re-layouts  34.2 us (16%)
  blocking collectives  23.1 us (11%)
  other arithmetic  12.8 us (6%)
  matrix products  8.09 us (4%)
    all_to_all x3, waiting for transfers between devices, exchange(): return lax.all_to_all(value, axes, 0, 0, tiled=True)  87 us
    all_to_all x3, starting transfers between devices, exchange(): return lax.all_to_all(value, axes, 0, 0, tiled=True)  33.1 us
    all_to_all x1, blocking collectives, exchange(): return lax.all_to_all(value, axes, 0, 0, tiled=True)  23.1 us
    reshape x1, local copies, waits for them, and re-layouts, body(): w_parts = w_out.reshape(chan_count, n_chip, 2, chan_count)  8.06 us
    reshape x2, local copies, waits for them, and re-layouts, banded(): tiled_taps[:, :tok_rows * (tok_rows + length - 1)]  7.97 us
    unnamed x48, local copies, waits for them, and re-layouts  6.61 us
    ppermute x2, waiting for transfers between devices, from_behind(): lax.ppermute(value, axis, [(source, source + steps) for source in range(l...  5.08 us
    ppermute x2, starting transfers between devices, from_behind(): lax.ppermute(value, axis, [(source, source + steps) for source in range(l...  4.99 us
  transfers between devices with their start and end apart: 7, of which 5 were waited for; matrix products, arithmetic and copies ran while one was open for 15% of the time, Pallas kernels for 0%

profile of v1, /device:TPU:6, one launch (start us, length us, event | category | flops | bytes accessed | tf_op | source)
XLA Modules:
  0.0 216.0 jit_solution(9701684717000204312)
XLA Ops:
  0.7 0.9 broadcast_in_dim.19
  1.6 23.1 %all_to_all.20 = bf16[12,128,256]{2,1,0:T(8,128)(2,1)S(1)} all-to-all(bf16[12,128,256]{2,1,0:T(8,128)(2,1)S(1)} %broadcast_in_dim.19), channel_id=1, replica_groups=mesh['zh'=4,'y'=8,'zl'=3,'x'=4,'core'=2] {'zl','x'}, dimensions={0} | all-to-all | bytes 1572864 | tf_op jit(solution)/shard_map/all_to_all | solution.py:30
  24.7 1.9 collective-permute-start.2
  26.7 0.1 reduce.2
  27.0 0.6 copy.71
  27.6 3.4 %reshape.188 = bf16[16,128,255]{2,1,0:T(8,128)(2,1)S(1)} reshape(bf16[16,32640]{1,0:T(8,128)(2,1)S(1)} %slice.32) | data formatting | bytes 2088960 | tf_op jit(solution)/shard_map/reshape | solution.py:24
  31.3 1.3 broadcast_select_fusion
  33.0 1.5 copy-done
  34.5 1.8 fusion.13
  36.3 1.4 collective-permute-start.3
  37.8 5.1 %collective-permute-done.3 = bf16[127,256]{1,0:T(8,128)(2,1)S(1)} collective-permute-done((bf16[127,256]{1,0:T(8,128)(2,1)S(1)}, bf16[127,256]{1,0:T(8,128)(2,1)S(1)}, u32[]{:S(2)}, u32[]{:S(2)}) %collective-permute-start.3) | collective-permute-done | bytes 65056 | tf_op jit(solution)/shard_map/ppermute | solution.py:12
  43.0 0.4 fusion.5
  43.5 0.7 fusion.14
  44.2 3.6 %collective-permute-start = (bf16[127,256]{1,0:T(8,128)(2,1)S(1)}, bf16[127,256]{1,0:T(8,128)(2,1)S(1)}, u32[]{:S(2)}, u32[]{:S(2)}) collective-permute-start(bf16[127,256]{1,0:T(8,128)(2,1)S(1)} %slice.29), channel_id=1, source_target_pairs={{0,24},{24,48},{48,72},{72,96},{96,120},{120,144},{144,168},{168,1... | collective-permute-start | bytes 195080 | tf_op jit(solution)/shard_map/ppermute | solution.py:12
  47.8 0.7 compare_convert_fusion
  48.7 0.6 copy.70
  49.3 1.1 slice.30
  50.3 4.6 %reshape.182 = bf16[16,128,255]{2,1,0:T(8,128)(2,1)S(1)} reshape(bf16[16,32640]{1,0:T(8,128)(2,1)} %slice.30) | data formatting | bytes 2088960 | tf_op jit(solution)/shard_map/reshape | solution.py:24
  55.0 0.7 copy.62
  55.8 0.4 fusion.7
  56.3 1.0 convolution_convert_fusion
  57.4 0.2 copy.76
  57.6 0.7 copy-done.4
  58.2 1.8 convolution_multiply_fusion
  60.1 4.0 %reshape.192 = f32[16,32640]{1,0:T(8,128)} reshape(f32[16,128,255]{2,1,0:T(8,128)} %convolution_multiply_fusion) | data formatting | bytes 4177920 | tf_op jit(solution)/shard_map/reshape | solution.py:112
  64.1 1.7 concatenate.26
  65.8 0.6 copy.72
  66.7 0.1 copy.63
  66.8 0.1 copy.64
  67.0 2.0 fusion.1
  69.0 12.4 %all-to-all-start.2 = ((bf16[8,4,208,256]{3,2,1,0:T(8,128)(2,1)}), bf16[8,4,208,256]{3,2,1,0:T(8,128)(2,1)S(1)}, u32[]{:S(2)}, u32[]{:S(2)}) async-start(bf16[8,4,208,256]{3,2,1,0:T(8,128)(2,1)} %fusion.1), calls=%async_computation.2 | async-start | bytes 6815744 | tf_op jit(solution)/shard_map/all_to_all | solution.py:30
  81.4 8.1 %reshape.186 = bf16[256,12,2,256]{3,2,1,0:T(2,128)(2,1)} reshape(bf16[256,6144]{1,0:T(8,128)(2,1)} %param.12) | data formatting | bytes 6291456 | tf_op jit(solution)/shard_map/reshape | solution.py:92
  89.5 2.7 %fusion.2 = f32[128,12,2,256]{3,0,2,1:T(8,128)S(1)} fusion(bf16[256,12,2,256]{3,2,1,0:T(2,128)(2,1)} %reshape.186, f32[128,256]{1,0:T(8,128)S(1)} %copy.54, bf16[128,256]{1,0:T(8,128)(2,1)} %param.7), kind=kOutput, calls=%fused_computation.5 | convolution fusion | flops 402751488 | bytes 6488064 | tf_op jit(solution)/shard_map/tc,cjkn->jktn/dot_general | solution.py:93
  92.2 1.7 copy-done.1
  93.8 1.0 fusion.9
  94.8 1.9 collective-permute-start.1
  96.7 2.6 %collective-permute-done.1 = bf16[12,128,256]{2,1,0:T(8,128)(2,1)} collective-permute-done((bf16[12,128,256]{2,1,0:T(8,128)(2,1)}, bf16[12,128,256]{2,1,0:T(8,128)(2,1)}, u32[]{:S(2)}, u32[]{:S(2)}) %collective-permute-start.1) | collective-permute-done | bytes 786464 | tf_op jit(solution)/shard_map/ppermute | solution.py:34
  99.3 2.8 %fusion.4 = bf16[12,128,256]{2,1,0:T(8,128)(2,1)} fusion(bf16[12,128,256]{2,1,0:T(8,128)(2,1)} %collective-permute-done.1, f32[128,12,2,256]{3,0,2,1:T(8,128)} %copy-done.1, s32[]{:T(128)S(6)} %select_n.28), kind=kLoop, calls=%fused_computation.9 | loop fusion | flops 1179648 | bytes 3145732 | tf_op jit(solution)/shard_map/convert_element_type | solution.py:53
  102.1 58.7 %all-to-all-done.2 = bf16[8,4,208,256]{3,2,1,0:T(8,128)(2,1)S(1)} async-done(((bf16[8,4,208,256]{3,2,1,0:T(8,128)(2,1)}), bf16[8,4,208,256]{3,2,1,0:T(8,128)(2,1)S(1)}, u32[]{:S(2)}, u32[]{:S(2)}) %all-to-all-start.2) | async-done | bytes 3407904 | tf_op jit(solution)/shard_map/all_to_all | solution.py:30
  160.8 4.5 %all-to-all-start = ((bf16[12,128,256]{2,1,0:T(8,128)(2,1)}), bf16[12,128,256]{2,1,0:T(8,128)(2,1)}, u32[]{:S(2)}, u32[]{:S(2)}) async-start(bf16[12,128,256]{2,1,0:T(8,128)(2,1)} %fusion.4), calls=%async_computation | async-start | bytes 1572864 | tf_op jit(solution)/shard_map/all_to_all | solution.py:30
  165.3 1.3 reduce_sum.44
  166.7 13.8 %all-to-all-done = bf16[12,128,256]{2,1,0:T(8,128)(2,1)} async-done(((bf16[12,128,256]{2,1,0:T(8,128)(2,1)}), bf16[12,128,256]{2,1,0:T(8,128)(2,1)}, u32[]{:S(2)}, u32[]{:S(2)}) %all-to-all-start) | async-done | bytes 786464 | tf_op jit(solution)/shard_map/all_to_all | solution.py:30
  180.5 16.2 %all-to-all-start.3 = ((bf16[4,208,256]{2,1,0:T(8,128)(2,1)}), bf16[4,208,256]{2,1,0:T(8,128)(2,1)S(1)}, u32[]{:S(2)}, u32[]{:S(2)}) async-start(bf16[4,208,256]{2,1,0:T(8,128)(2,1)} %reduce_sum.44), calls=%async_computation.3 | async-start | bytes 851968 | tf_op jit(solution)/shard_map/all_to_all | solution.py:30
  196.6 1.5 multiply_convert_fusion
  198.2 1.9 reduce_sum.42
  200.1 14.5 %all-to-all-done.3 = bf16[4,208,256]{2,1,0:T(8,128)(2,1)S(1)} async-done(((bf16[4,208,256]{2,1,0:T(8,128)(2,1)}), bf16[4,208,256]{2,1,0:T(8,128)(2,1)S(1)}, u32[]{:S(2)}, u32[]{:S(2)}) %all-to-all-start.3) | async-done | bytes 426016 | tf_op jit(solution)/shard_map/all_to_all | solution.py:30
  214.6 0.7 fusion.17
  215.4 0.7 copy.66
  (71 shorter events, 1.8 us)
Async XLA Ops:
  0.6 26.0 %copy-start.9 = (s32[16]{0:T(128)S(1)}, s32[16]{0:T(128)}, u32[]{:S(2)}) copy-start(s32[16]{0:T(128)} %param.11) | copy-start | bytes 196
  0.6 26.2 %copy-start.8 = (bf16[16,128]{1,0:T(8,128)(2,1)S(1)}, bf16[16,128]{1,0:T(8,128)(2,1)}, u32[]{:S(2)}) copy-start(bf16[16,128]{1,0:T(8,128)(2,1)} %param.10) | copy-start | bytes 12292
  24.7 6.6 %collective-permute-start.2 = (bf16[12,128,256]{2,1,0:T(8,128)(2,1)S(1)}, bf16[12,128,256]{2,1,0:T(8,128)(2,1)}, u32[]{:S(2)}, u32[]{:S(2)}) collective-permute-start(bf16[12,128,256]{2,1,0:T(8,128)(2,1)S(1)} %all_to_all.20), channel_id=1, source_target_pairs={{0,1},{1,0},{2,3},{3,2},{4,5},{5,4},{6,7},{7,6},{8,9},{9,8},{10,11... | collective-permute-start | bytes 2359304 | tf_op jit(solution)/shard_map/ppermute | solution.py:34
  31.3 1.7 copy-start.2
  32.6 1.9 copy-start
  36.3 7.1 %copy-start.6 = (bf16[128,256]{1,0:T(8,128)(2,1)S(1)}, bf16[128,256]{1,0:T(8,128)(2,1)}, u32[]{:S(2)}) copy-start(bf16[128,256]{1,0:T(8,128)(2,1)} %param.8) | copy-start | bytes 196612
  36.3 7.1 %copy-start.7 = (bf16[128,256]{1,0:T(8,128)(2,1)S(1)}, bf16[128,256]{1,0:T(8,128)(2,1)}, u32[]{:S(2)}) copy-start(bf16[128,256]{1,0:T(8,128)(2,1)} %param.9) | copy-start | bytes 196612
  36.3 6.5 %collective-permute-start.3 = (bf16[127,256]{1,0:T(8,128)(2,1)S(1)}, bf16[127,256]{1,0:T(8,128)(2,1)S(1)}, u32[]{:S(2)}, u32[]{:S(2)}) collective-permute-start(bf16[127,256]{1,0:T(8,128)(2,1)S(1)} %bitcast.157), channel_id=1, source_target_pairs={{24,0},{48,24},{72,48},{96,72},{120,96},{144,120},{168,144},{192,1... | collective-permute-start | bytes 195080 | tf_op jit(solution)/shard_map/ppermute | solution.py:12
  44.2 11.5 %collective-permute-start = (bf16[127,256]{1,0:T(8,128)(2,1)S(1)}, bf16[127,256]{1,0:T(8,128)(2,1)S(1)}, u32[]{:S(2)}, u32[]{:S(2)}) collective-permute-start(bf16[127,256]{1,0:T(8,128)(2,1)S(1)} %slice.29), channel_id=1, source_target_pairs={{0,24},{24,48},{48,72},{72,96},{96,120},{120,144},{144,168},{168,1... | collective-permute-start | bytes 195080 | tf_op jit(solution)/shard_map/ppermute | solution.py:12
  54.9 1.4 copy-start.3
  57.3 0.9 copy-start.4
  57.4 0.9 copy-start.5
  69.0 91.8 %all-to-all-start.2 = ((bf16[8,4,208,256]{3,2,1,0:T(8,128)(2,1)}), bf16[8,4,208,256]{3,2,1,0:T(8,128)(2,1)S(1)}, u32[]{:S(2)}, u32[]{:S(2)}) async-start(bf16[8,4,208,256]{3,2,1,0:T(8,128)(2,1)} %fusion.1), calls=%async_computation.2 | async-start | bytes 6815744 | tf_op jit(solution)/shard_map/all_to_all | solution.py:30
  92.2 1.7 copy-start.1
  94.8 4.5 %collective-permute-start.1 = (bf16[12,128,256]{2,1,0:T(8,128)(2,1)}, bf16[12,128,256]{2,1,0:T(8,128)(2,1)}, u32[]{:S(2)}, u32[]{:S(2)}) collective-permute-start(bf16[12,128,256]{2,1,0:T(8,128)(2,1)} %fusion.9), channel_id=1, source_target_pairs={{0,1},{1,0},{2,3},{3,2},{4,5},{5,4},{6,7},{7,6},{8,9},{9,8},{10,11... | collective-permute-start | bytes 2359304 | tf_op jit(solution)/shard_map/ppermute | solution.py:34
  160.8 19.6 %all-to-all-start = ((bf16[12,128,256]{2,1,0:T(8,128)(2,1)}), bf16[12,128,256]{2,1,0:T(8,128)(2,1)}, u32[]{:S(2)}, u32[]{:S(2)}) async-start(bf16[12,128,256]{2,1,0:T(8,128)(2,1)} %fusion.4), calls=%async_computation | async-start | bytes 1572864 | tf_op jit(solution)/shard_map/all_to_all | solution.py:30
  180.5 34.1 %all-to-all-start.3 = ((bf16[4,208,256]{2,1,0:T(8,128)(2,1)}), bf16[4,208,256]{2,1,0:T(8,128)(2,1)S(1)}, u32[]{:S(2)}, u32[]{:S(2)}) async-start(bf16[4,208,256]{2,1,0:T(8,128)(2,1)} %reduce_sum.44), calls=%async_computation.3 | async-start | bytes 851968 | tf_op jit(solution)/shard_map/all_to_all | solution.py:30

commit v2 on v1

v2 whole, which is shorter than its diff:
```python
import jax
import jax.numpy as jnp
from jax import lax
from jax.experimental import pallas as pl
from jax.experimental.pallas import tpu as pltpu
from jax.sharding import Mesh, PartitionSpec as P

SEQ, CHAN, CHIPS = ("zh", "y"), ("zl", "x", "core"), ("zl", "x")
F32, BF16 = jnp.float32, jnp.bfloat16
SMEM = pl.BlockSpec(memory_space=pltpu.SMEM)
VMEM = pl.BlockSpec(memory_space=pltpu.VMEM)


def iota(shape, axis):
    return lax.broadcasted_iota(jnp.int32, shape, axis)


def start_at(where_ref, count, pos):
    found, running = jnp.zeros(pos.shape, jnp.int32), jnp.int32(0)
    for doc in range(count):
        found = jnp.where(pos >= running, running, found)
        running = running + where_ref[doc]
    return found


def forward_mask(where_ref, docs, rows, flipped=False):
    first = where_ref[docs]
    own = first + (rows - 1 - iota((rows, 2 * rows), 0) if flipped else iota((rows, 2 * rows), 0))
    source = first - rows + iota((rows, 2 * rows), 1)
    return source >= start_at(where_ref, docs, own)


def backward_mask(where_ref, docs, rows):
    first = where_ref[docs]
    start = start_at(where_ref, docs, first + iota((8, 2 * rows), 1))[0:1]
    return first + iota((rows, 2 * rows), 0) >= start


def spread(row, rows):
    return pltpu.roll(jnp.broadcast_to(row, (rows, row.shape[1])), 0, 1, stride=1, stride_axis=0)


def apply_bands(taps_ref, mask, ext, rows, half, per_group):
    member = iota((rows, half), 1) // per_group
    outs = []
    for side in range(ext.shape[1] // half):
        total = jnp.zeros((rows, half), F32)
        piece = ext[:, side * half : (side + 1) * half]
        for group in range(half // per_group):
            index = side * (half // per_group) + group
            band = jnp.where(mask, spread(taps_ref[index : index + 1, :], rows), 0.0).astype(BF16)
            value = jnp.dot(band, piece, preferred_element_type=F32)
            total = jnp.where(member == group, value, total)
        outs.append(total)
    return outs


def filter_kernel(docs, per_group, where_ref, taps_ref, prev_ref, prod_ref, q_ref, filt_ref, gated_ref):
    rows, half = prod_ref.shape[0], 128
    mask = forward_mask(where_ref, docs, rows)
    ext = jnp.concatenate([prev_ref[...], prod_ref[...]], axis=0)
    for side, total in enumerate(apply_bands(taps_ref, mask, ext, rows, half, per_group)):
        lanes = slice(side * half, (side + 1) * half)
        filt_ref[:, lanes] = total
        gated_ref[:, lanes] = (q_ref[:, lanes].astype(F32) * total).astype(BF16)


def grad_kernel(
    docs, per_group, where_ref, mine_ref, other_ref, w_ref, q_ref, filt_ref, gated_ref, prev_ref, prod_ref,
    gate_ref, query_ref, pay_ref, sums,
):
    rows, half = prod_ref.shape[0], 128
    blocks, part, wide = mine_ref.shape
    core = where_ref[docs + 1]
    for ref, at in ((mine_ref, core), (other_ref, 1 - core)):
        total = jnp.zeros((part, w_ref.shape[0]), F32)
        for block in range(blocks):
            total = total + lax.dot_general(
                ref[block], w_ref[:, block * wide : (block + 1) * wide], (((1,), (1,)), ((), ())),
                preferred_element_type=F32,
            )
        sums[pl.ds(pl.multiple_of(at * part, part), part), :] = total
    grad_in = sums[...]
    gate = (grad_in * q_ref[...].astype(F32)).astype(BF16)
    gate_ref[...] = gate
    query_ref[...] = (grad_in * filt_ref[...]).astype(BF16)
    mask = forward_mask(where_ref, docs, rows, True)
    mirror = (iota((rows, rows), 0) + iota((rows, rows), 1) == rows - 1).astype(F32).astype(BF16)
    flipped = jnp.dot(mirror, gate, preferred_element_type=F32)
    member = iota((rows, half), 1) // per_group
    lines = []
    for side in range(prod_ref.shape[1] // half):
        lanes = slice(side * half, (side + 1) * half)
        ext = jnp.concatenate([prev_ref[:, lanes], prod_ref[:, lanes]], axis=0)
        for group in range(half // per_group):
            chosen = jnp.where(member == group, flipped[:, lanes], 0.0).astype(BF16)
            pairs = lax.dot_general(chosen, ext, (((1,), (1,)), ((), ())), preferred_element_type=F32)
            pairs = jnp.where(mask, pairs, 0.0)
            pairs = pltpu.roll(pairs, rows + 1, 1, stride=1, stride_axis=0)
            lines.append(jnp.sum(pairs, axis=0, keepdims=True))
    taps = jnp.concatenate(lines, axis=0).astype(BF16)
    for peer in range(pay_ref.shape[0]):
        pay_ref[peer, :rows, :] = gated_ref[...]
        pay_ref[peer, rows:, :] = taps


def back_kernel(docs, per_group, where_ref, taps_ref, gate_ref, next_ref, k_ref, v_ref, key_ref, value_ref):
    rows, half = gate_ref.shape[0], 128
    mask = backward_mask(where_ref, docs, rows)
    ext = jnp.concatenate([gate_ref[...], next_ref[...]], axis=0)
    for side, total in enumerate(apply_bands(taps_ref, mask, ext, rows, half, per_group)):
        lanes = slice(side * half, (side + 1) * half)
        key_ref[:, lanes] = (total * v_ref[:, lanes].astype(F32)).astype(BF16)
        value_ref[:, lanes] = (total * k_ref[:, lanes].astype(F32)).astype(BF16)


def pick_kernel(unit, columns, rows_ref, out_ref):
    peers, part, wide = out_ref.shape
    block, lanes = rows_ref.shape[2], 128
    per_chunk, chunks = columns // unit, wide // columns
    low = iota((part, lanes), 1) < unit

    def half(index, upper):
        start = index * unit // lanes * lanes
        tile = rows_ref[start // block, :, start % block : start % block + lanes].astype(F32)
        return tile if (index % 2 == 1) == upper else pltpu.roll(tile, unit, 1)

    for peer in range(peers):
        units = [(c * peers + peer) * per_chunk + u for c in range(chunks) for u in range(per_chunk)]
        for tile in range(wide // lanes):
            a, b = units[2 * tile], units[2 * tile + 1]
            out_ref[peer, :, tile * lanes : (tile + 1) * lanes] = jnp.where(low, half(a, False), half(b, True)).astype(BF16)


def project_sent(docs, where_ref, gated_ref, w_ref, out_ref):
    blocks, _, width = out_ref.shape
    core = 1 - where_ref[docs + 1]
    for block in range(blocks):
        lanes = pl.ds(pl.multiple_of((2 * block + core) * width, width), width)
        out_ref[block] = jnp.dot(gated_ref[...], w_ref[:, lanes], preferred_element_type=F32).astype(BF16)


def project_kept(docs, where_ref, gated_ref, w_ref, came_ref, out_ref):
    blocks, _, width = out_ref.shape
    core = where_ref[docs + 1]
    for block in range(blocks):
        lanes = pl.ds(pl.multiple_of((2 * block + core) * width, width), width)
        total = jnp.dot(gated_ref[...], w_ref[:, lanes], preferred_element_type=F32)
        out_ref[block] = (total + came_ref[block].astype(F32)).astype(BF16)


def call(kernel, outs, ins, scratch=(), name=None):
    return pl.pallas_call(
        kernel,
        out_shape=outs,
        in_specs=[SMEM if a.dtype == jnp.int32 else VMEM for a in ins],
        out_specs=jax.tree.map(lambda _: VMEM, outs),
        scratch_shapes=list(scratch),
        name=name,
    )(*ins)


def like(shape, dtype=BF16):
    return jax.ShapeDtypeStruct(shape, dtype)


def shifted(value, axis, steps):
    count = lax.axis_size(axis)
    leading, last = (max(0, -steps), min(count, count - steps))
    return lax.ppermute(value, axis, [(source, source + steps) for source in range(leading, last)])


def exchange(value, axes):
    return lax.all_to_all(value, axes, 0, 0, tiled=True)


def swap_cores(value):
    return lax.ppermute(value, "core", [(0, 1), (1, 0)])


def body(query_in, key_in, value_in, filters, doc_lengths, w_out, cotangent):
    rows, width = query_in.shape
    groups, length = filters.shape
    part, per_group, docs = rows // 2, width // groups, doc_lengths.shape[0]
    n_zh, n_y, n_chip = lax.axis_size("zh"), lax.axis_size("y"), lax.axis_size(CHIPS)
    core, place = lax.axis_index("core"), lax.axis_index(SEQ)
    columns = n_chip * 2 * width // (n_zh * n_y)
    where = jnp.concatenate([doc_lengths, jnp.stack([place * rows, core]).astype(jnp.int32)])

    halves = cotangent.reshape(2, part, width)
    kept = lax.dynamic_index_in_dim(halves, core, 0, keepdims=False)
    came = swap_cores(lax.dynamic_index_in_dim(halves, 1 - core, 0, keepdims=False))
    both = jnp.where(core == 0, jnp.concatenate([kept, came], 1), jnp.concatenate([came, kept], 1))
    mine = exchange(jnp.broadcast_to(both[None], (n_chip, part, 2 * width)), CHIPS)
    picked = call(lambda *r: pick_kernel(64, columns, *r), like((n_y, part, n_zh * columns)), [mine], name="pick")
    picked = exchange(picked, "y")
    other = swap_cores(mine)

    product = (key_in.astype(F32) * value_in.astype(F32)).astype(BF16)
    prev = shifted(product, SEQ, 1)
    taps = filters.astype(F32)
    zeros = jnp.zeros((groups, 2 * rows - length), F32)
    ahead = jnp.concatenate([zeros[:, :1], jnp.flip(taps, 1), zeros[:, 1:]], axis=1)
    behind = jnp.concatenate([taps, zeros], axis=1)
    filtered, gated = call(
        lambda *r: filter_kernel(docs, per_group, *r), (like((rows, width), F32), like((rows, width))),
        [where, ahead, prev, product, query_in], name="filter",
    )
    gate, grad_query, pay = call(
        lambda *r: grad_kernel(docs, per_group, *r),
        (like((rows, width)), like((rows, width)), like((n_y, rows + groups, width))),
        [where, mine, other, w_out, query_in, filtered, gated, prev, product],
        [pltpu.VMEM((rows, width), F32)], name="grad",
    )
    gathered = exchange(pay, "y")
    picked_other = swap_cores(picked)

    sent = call(lambda *r: project_sent(docs, *r), like((n_chip, rows, width)), [where, gated, w_out], name="sent")
    pair = call(
        lambda *r: project_kept(docs, *r), like((n_chip, rows, width)), [where, gated, w_out, swap_cores(sent)], name="kept"
    )
    block_out = jnp.sum(exchange(pair, CHIPS).astype(F32), axis=0).astype(BF16)

    following = shifted(gate, SEQ, -1)
    grad_key, grad_value = call(
        lambda *r: back_kernel(docs, per_group, *r), (like((rows, width)), like((rows, width))),
        [where, behind, gate, following, key_in, value_in], name="back",
    )

    upper, lower = gathered[:, :part], gathered[:, part:rows]
    weight = jnp.einsum("ytn,ytc->nc", picked, jnp.where(core == 0, upper, lower), preferred_element_type=F32)
    weight += jnp.einsum("ytn,ytc->nc", picked_other, jnp.where(core == 0, lower, upper), preferred_element_type=F32)
    tap_terms = jnp.sum(gathered[:, rows:].astype(F32), axis=0).astype(BF16)
    terms = jnp.concatenate(
        [weight.astype(BF16).reshape(n_zh, columns, width), jnp.broadcast_to(tap_terms[None], (n_zh, groups, width))], axis=1
    )
    total = jnp.sum(exchange(terms, "zh").astype(F32), axis=0)
    owned = length // (n_zh * n_y)
    tap_sum = lax.dynamic_slice_in_dim(total[columns:], rows + 1 - (place + 1) * owned, owned, 1)
    return (block_out, grad_query, grad_key, grad_value, total[:columns].T.astype(BF16), jnp.flip(tap_sum, 1))


def build(fine):
    both, rows = P(SEQ, CHAN), P(CHAN, None)
    return jax.shard_map(
        body,
        mesh=fine,
        in_specs=(both, both, both, rows, P(), rows, both),
        out_specs=(both, both, both, both, P(CHAN, SEQ), P(CHAN, SEQ)),
        check_vma=False,
    )


def solution(mesh):
    return build(Mesh(mesh.devices.reshape(4, 8, 3, 4, 2), SEQ + CHAN))
```

time: 217 us -> 152 us (0.70)
  the two profiles are of different devices: /device:TPU:6 before, /device:TPU:121 now
where the time goes in v2:
time: 152 us
  starting transfers between devices  64.3 us (42%)
  waiting for transfers between devices  35.1 us (23%)
  blocking collectives  21.9 us (14%)
  Pallas kernels  19.5 us (13%)
  local copies, waits for them, and re-layouts  6.18 us (4%)
  other arithmetic  2.98 us (2%)
    all_to_all x4, starting transfers between devices, exchange(): return lax.all_to_all(value, axes, 0, 0, tiled=True)  33.2 us
    ppermute x2, waiting for transfers between devices, shifted(): lax.ppermute(value, axis, [(source, source + steps) for source in range(l...  26.8 us
    all_to_all x1, blocking collectives, exchange(): return lax.all_to_all(value, axes, 0, 0, tiled=True)  21.9 us
    pallas_call x6, Pallas kernels, call(): pl.pallas_call(kernel, out_shape=outs, in_specs=[SMEM if a.dtype == jnp.i...  19.5 us
    ppermute x2, starting transfers between devices, shifted(): lax.ppermute(value, axis, [(source, source + steps) for source in range(l...  16.5 us
    ppermute x4, starting transfers between devices, swap_cores(): return lax.ppermute(value, 'core', [(0, 1), (1, 0)])  14.7 us
    ppermute x4, waiting for transfers between devices, swap_cores(): return lax.ppermute(value, 'core', [(0, 1), (1, 0)])  4.37 us
    all_to_all x4, waiting for transfers between devices, exchange(): return lax.all_to_all(value, axes, 0, 0, tiled=True)  3.95 us
  transfers between devices with their start and end apart: 10, of which 6 were waited for; matrix products, arithmetic and copies ran while one was open for 3% of the time, Pallas kernels for 11%

profile of v2, /device:TPU:121, one launch (start us, length us, event | category | flops | bytes accessed | tf_op | source)
XLA Modules:
  0.0 151.7 jit_solution(11669509394743893508)
XLA Ops:
  0.6 0.0 copy-start.6
  0.6 0.0 copy-start.5
  0.7 0.8 dynamic-slice_bitcast_fusion.1
  1.5 2.6 %collective-permute-start.2 = (bf16[64,256]{1,0:T(8,128)(2,1)S(1)}, bf16[64,256]{1,0:T(8,128)(2,1)S(1)}, u32[]{:S(2)}, u32[]{:S(2)}) collective-permute-start(bf16[64,256]{1,0:T(8,128)(2,1)S(1)} %get-tuple-element.33), channel_id=1, source_target_pairs={{0,1},{1,0},{2,3},{3,2},{4,5},{5,4},{6,7},{7,6},{8,9},{9,8},{10,11... | collective-permute-start | bytes 98312 | tf_op jit(solution)/shard_map/ppermute | solution.py:178
  4.1 0.8 collective-permute-done.2
  4.9 0.1 broadcast_in_dim.4
  5.0 21.9 %all_to_all.25.r_1_.r_0_ = bf16[12,64,512]{2,1,0:T(8,128)(2,1)} all-to-all(bf16[12,64,512]{2,1,0:T(8,128)(2,1)S(1)} %broadcast_in_dim.4), channel_id=1, replica_groups=mesh['zh'=4,'y'=8,'zl'=3,'x'=4,'core'=2] {'zl','x'}, dimensions={0} | all-to-all | bytes 1572864 | tf_op jit(solution)/shard_map/all_to_all | solution.py:174
  26.9 2.4 %pick.1 = bf16[8,64,768]{2,1,0:T(8,128)(2,1)} custom-call(bf16[12,64,512]{2,1,0:T(8,128)(2,1)} %all_to_all.25.r_1_.r_0_), custom_call_target="tpu_custom_call" | custom-call | tf_op jit(solution)/shard_map/pick/pallas_call | solution.py:153
  29.3 7.9 %all-to-all-start.2 = ((bf16[8,64,768]{2,1,0:T(8,128)(2,1)}), bf16[8,64,768]{2,1,0:T(8,128)(2,1)S(1)}, u32[]{:S(2)}, u32[]{:S(2)}) async-start(bf16[8,64,768]{2,1,0:T(8,128)(2,1)} %pick.1), calls=%async_computation.2 | async-start | bytes 1572864 | tf_op jit(solution)/shard_map/all_to_all | solution.py:174
  37.2 3.6 %collective-permute-start.3 = (bf16[12,64,512]{2,1,0:T(8,128)(2,1)S(1)}, bf16[12,64,512]{2,1,0:T(8,128)(2,1)S(1)}, u32[]{:S(2)}, u32[]{:S(2)}) collective-permute-start(bf16[12,64,512]{2,1,0:T(8,128)(2,1)S(1)} %copy-done), channel_id=1, source_target_pairs={{0,1},{1,0},{2,3},{3,2},{4,5},{5,4},{6,7},{7,6},{8,9},{9,8},{10,11... | collective-permute-start | bytes 2359304 | tf_op jit(solution)/shard_map/ppermute | solution.py:178
  40.9 0.0 copy-start.3
  40.9 8.4 %collective-permute-start = (bf16[128,256]{1,0:T(8,128)(2,1)S(1)}, bf16[128,256]{1,0:T(8,128)(2,1)S(1)}, u32[]{:S(2)}, u32[]{:S(2)}) collective-permute-start(bf16[128,256]{1,0:T(8,128)(2,1)S(1)} %multiply_convert_fusion.r_3_.r_8_), channel_id=1, source_target_pairs={{0,24},{24,48},{48,72},{72,96},{96,120},{120,144},{144,168},{168,1... | collective-permute-start | bytes 196616 | tf_op jit(solution)/shard_map/ppermute | solution.py:170
  49.3 0.1 rev.8
  49.4 0.1 pad.9.clone
  49.5 0.7 maximum_maximum_fusion.r_1_
  50.2 0.7 pad_add_fusion.r_0_
  50.8 5.1 %collective-permute-done.r_2_.r_7_ = bf16[128,256]{1,0:T(8,128)(2,1)S(1)} collective-permute-done((bf16[128,256]{1,0:T(8,128)(2,1)S(1)}, bf16[128,256]{1,0:T(8,128)(2,1)S(1)}, u32[]{:S(2)}, u32[]{:S(2)}) %collective-permute-start) | collective-permute-done | bytes 65568 | tf_op jit(solution)/shard_map/ppermute | solution.py:170
  55.9 0.6 copy-done.4
  56.6 2.1 %filter.1 = (f32[128,256]{1,0:T(8,128)}, bf16[128,256]{1,0:T(8,128)(2,1)}) custom-call(s32[18]{0:T(128)} %pad_add_fusion.r_0_, f32[16,256]{1,0:T(8,128)} %maximum_maximum_fusion.r_1_, bf16[128,256]{1,0:T(8,128)(2,1)} %copy-done.4, bf16[128,256]{1,0:T(8,128)(2,1)} %copy-done.3, bf16[128,256]{1,0:T(8,128)(2,1)} %r_4_.4), custom_call_target="tpu_custom_call" | custom-call | tf_op jit(solution)/shard_map/filter/pallas_call | solution.py:153
  58.7 0.0 collective-permute-done.3.r_2_
  58.7 0.9 copy-done.2
  59.6 6.2 %grad.1 = (bf16[128,256]{1,0:T(8,128)(2,1)}, bf16[128,256]{1,0:T(8,128)(2,1)}, bf16[8,144,256]{2,1,0:T(8,128)(2,1)}) custom-call(s32[18]{0:T(128)} %pad_add_fusion.r_0_, bf16[12,64,512]{2,1,0:T(8,128)(2,1)} %all_to_all.25.r_1_.r_0_, bf16[12,64,512]{2,1,0:T(8,128)(2,1)} %copy-done.2, bf16[256,6144]{1,0:T(8,128)(2,1)} %r_3_.1, bf16[128,256]{1,0:T(8,128)(2,1)} %r_4_.4, ...), custom_call_target="tpu_custom_call" | custom-call | tf_op jit(solution)/shard_map/grad/pallas_call | solution.py:153
  65.8 7.8 %all-to-all-start.3 = ((bf16[8,144,256]{2,1,0:T(8,128)(2,1)}), bf16[8,144,256]{2,1,0:T(8,128)(2,1)S(1)}, u32[]{:S(2)}, u32[]{:S(2)}) async-start(bf16[8,144,256]{2,1,0:T(8,128)(2,1)} %get-tuple-element.19), calls=%async_computation.3 | async-start | bytes 1179648 | tf_op jit(solution)/shard_map/all_to_all | solution.py:174
  73.6 3.2 %sent.1 = bf16[12,128,256]{2,1,0:T(8,128)(2,1)} custom-call(s32[18]{0:T(128)} %pad_add_fusion.r_0_, bf16[128,256]{1,0:T(8,128)(2,1)} %get-tuple-element.13.r_1_.r_6_, bf16[256,6144]{1,0:T(8,128)(2,1)} %r_3_.1), custom_call_target="tpu_custom_call" | custom-call | tf_op jit(solution)/shard_map/sent/pallas_call | solution.py:153
  76.8 3.0 %collective-permute-start.1 = (bf16[12,128,256]{2,1,0:T(8,128)(2,1)}, bf16[12,128,256]{2,1,0:T(8,128)(2,1)S(1)}, u32[]{:S(2)}, u32[]{:S(2)}) collective-permute-start(bf16[12,128,256]{2,1,0:T(8,128)(2,1)} %sent.1), channel_id=1, source_target_pairs={{0,1},{1,0},{2,3},{3,2},{4,5},{5,4},{6,7},{7,6},{8,9},{9,8},{10,11... | collective-permute-start | bytes 2359304 | tf_op jit(solution)/shard_map/ppermute | solution.py:178
  79.8 2.1 %collective-permute-done.1.r_3_ = bf16[12,128,256]{2,1,0:T(8,128)(2,1)S(1)} collective-permute-done((bf16[12,128,256]{2,1,0:T(8,128)(2,1)}, bf16[12,128,256]{2,1,0:T(8,128)(2,1)S(1)}, u32[]{:S(2)}, u32[]{:S(2)}) %collective-permute-start.1) | collective-permute-done | bytes 786464 | tf_op jit(solution)/shard_map/ppermute | solution.py:178
  81.9 0.9 copy-done.1
  82.8 3.4 %kept.1 = bf16[12,128,256]{2,1,0:T(8,128)(2,1)} custom-call(s32[18]{0:T(128)} %pad_add_fusion.r_0_, bf16[128,256]{1,0:T(8,128)(2,1)} %get-tuple-element.13.r_1_.r_6_, bf16[256,6144]{1,0:T(8,128)(2,1)} %r_3_.1, bf16[12,128,256]{2,1,0:T(8,128)(2,1)} %copy-done.1), custom_call_target="tpu_custom_call" | custom-call | tf_op jit(solution)/shard_map/kept/pallas_call | solution.py:153
  86.2 4.2 %all-to-all-start = ((bf16[12,128,256]{2,1,0:T(8,128)(2,1)}), bf16[12,128,256]{2,1,0:T(8,128)(2,1)S(1)}, u32[]{:S(2)}, u32[]{:S(2)}) async-start(bf16[12,128,256]{2,1,0:T(8,128)(2,1)} %kept.1), calls=%async_computation | async-start | bytes 1572864 | tf_op jit(solution)/shard_map/all_to_all | solution.py:174
  90.4 5.5 %collective-permute-start.5 = (bf16[8,64,768]{2,1,0:T(8,128)(2,1)S(1)}, bf16[8,64,768]{2,1,0:T(8,128)(2,1)S(1)}, u32[]{:S(2)}, u32[]{:S(2)}) collective-permute-start(bf16[8,64,768]{2,1,0:T(8,128)(2,1)S(1)} %all-to-all-done.2), channel_id=1, source_target_pairs={{0,1},{1,0},{2,3},{3,2},{4,5},{5,4},{6,7},{7,6},{8,9},{9,8},{10,11... | collective-permute-start | bytes 2359304 | tf_op jit(solution)/shard_map/ppermute | solution.py:178
  96.0 0.4 convolution_bitcast_fusion.1
  96.4 0.0 copy-start.7
  96.4 1.4 collective-permute-done.5
  97.9 0.4 fusion.1
  98.3 0.8 pad_maximum_fusion
  99.1 3.9 %all-to-all-done = bf16[12,128,256]{2,1,0:T(8,128)(2,1)S(1)} async-done(((bf16[12,128,256]{2,1,0:T(8,128)(2,1)}), bf16[12,128,256]{2,1,0:T(8,128)(2,1)S(1)}, u32[]{:S(2)}, u32[]{:S(2)}) %all-to-all-start) | async-done | bytes 786464 | tf_op jit(solution)/shard_map/all_to_all | solution.py:174
  103.0 13.2 %all-to-all-start.4 = ((bf16[4,208,256]{2,1,0:T(8,128)(2,1)}), bf16[4,208,256]{2,1,0:T(8,128)(2,1)S(1)}, u32[]{:S(2)}, u32[]{:S(2)}) async-start(bf16[4,208,256]{2,1,0:T(8,128)(2,1)} %pad_maximum_fusion), calls=%async_computation.4 | async-start | bytes 851968 | tf_op jit(solution)/shard_map/all_to_all | solution.py:174
  116.3 8.1 %collective-permute-start.4 = (bf16[128,256]{1,0:T(8,128)(2,1)S(1)}, bf16[128,256]{1,0:T(8,128)(2,1)S(1)}, u32[]{:S(2)}, u32[]{:S(2)}) collective-permute-start(bf16[128,256]{1,0:T(8,128)(2,1)S(1)} %copy-done.7), channel_id=1, source_target_pairs={{24,0},{48,24},{72,48},{96,72},{120,96},{144,120},{168,144},{192,1... | collective-permute-start | bytes 196616 | tf_op jit(solution)/shard_map/ppermute | solution.py:170
  124.4 0.6 concatenate.33.r_1_
  125.0 0.7 reduce_sum.33
  125.7 21.7 %collective-permute-done.4.r_3_ = bf16[128,256]{1,0:T(8,128)(2,1)S(1)} collective-permute-done((bf16[128,256]{1,0:T(8,128)(2,1)S(1)}, bf16[128,256]{1,0:T(8,128)(2,1)S(1)}, u32[]{:S(2)}, u32[]{:S(2)}) %collective-permute-start.4) | collective-permute-done | bytes 65568 | tf_op jit(solution)/shard_map/ppermute | solution.py:170
  147.4 0.6 copy-done.8
  148.0 2.1 %back.1 = (bf16[128,256]{1,0:T(8,128)(2,1)}, bf16[128,256]{1,0:T(8,128)(2,1)}) custom-call(s32[18]{0:T(128)} %pad_add_fusion.r_0_, f32[16,256]{1,0:T(8,128)} %concatenate.33.r_1_, bf16[128,256]{1,0:T(8,128)(2,1)} %get-tuple-element.16.r_2_, bf16[128,256]{1,0:T(8,128)(2,1)} %copy-done.8, bf16[128,256]{1,0:T(8,128)(2,1)} %r_4_.5, bf16[128,256]{1,0:T(8,128)(2,1)} %r_5_.1), custom_call_target="tpu_custom_call" | custom-call | tf_op jit(solution)/shard_map/back/pallas_call | solution.py:153
  150.1 0.1 convert_reduce_fusion
  150.2 0.7 fusion.10
  150.9 0.1 constant_dynamic-slice_fusion
  150.9 0.1 rev.9
  151.0 0.7 copy.14
  (24 shorter events, 0.1 us)
Async XLA Ops:
  0.6 40.2 %copy-start.6 = (bf16[128,256]{1,0:T(8,128)(2,1)S(1)}, bf16[128,256]{1,0:T(8,128)(2,1)}, u32[]{:S(2)}) copy-start(bf16[128,256]{1,0:T(8,128)(2,1)} %r_4_.5) | copy-start | bytes 196612
  0.6 40.2 %copy-start.5 = (bf16[128,256]{1,0:T(8,128)(2,1)S(1)}, bf16[128,256]{1,0:T(8,128)(2,1)}, u32[]{:S(2)}) copy-start(bf16[128,256]{1,0:T(8,128)(2,1)} %r_5_.1) | copy-start | bytes 196612
  0.7 48.7 %copy-start.9 = (bf16[16,128]{1,0:T(8,128)(2,1)S(1)}, bf16[16,128]{1,0:T(8,128)(2,1)}, u32[]{:S(2)}) copy-start(bf16[16,128]{1,0:T(8,128)(2,1)} %param.10) | copy-start | bytes 12292
  0.7 49.5 %copy-start.10 = (s32[16]{0:T(128)S(1)}, s32[16]{0:T(128)}, u32[]{:S(2)}) copy-start(s32[16]{0:T(128)} %param.11) | copy-start | bytes 196
  1.5 3.4 %collective-permute-start.2 = (bf16[64,256]{1,0:T(8,128)(2,1)S(1)}, bf16[64,256]{1,0:T(8,128)(2,1)S(1)}, u32[]{:S(2)}, u32[]{:S(2)}) collective-permute-start(bf16[64,256]{1,0:T(8,128)(2,1)S(1)} %get-tuple-element.33), channel_id=1, source_target_pairs={{0,1},{1,0},{2,3},{3,2},{4,5},{5,4},{6,7},{7,6},{8,9},{9,8},{10,11... | collective-permute-start | bytes 98312 | tf_op jit(solution)/shard_map/ppermute | solution.py:178
  26.9 10.3 %copy-start = (bf16[12,64,512]{2,1,0:T(8,128)(2,1)S(1)}, bf16[12,64,512]{2,1,0:T(8,128)(2,1)}, u32[]{:S(2)}) copy-start(bf16[12,64,512]{2,1,0:T(8,128)(2,1)} %all_to_all.25.r_1_.r_0_) | copy-start | bytes 2359300
  29.3 36.5 %all-to-all-start.2 = ((bf16[8,64,768]{2,1,0:T(8,128)(2,1)}), bf16[8,64,768]{2,1,0:T(8,128)(2,1)S(1)}, u32[]{:S(2)}, u32[]{:S(2)}) async-start(bf16[8,64,768]{2,1,0:T(8,128)(2,1)} %pick.1), calls=%async_computation.2 | async-start | bytes 1572864 | tf_op jit(solution)/shard_map/all_to_all | solution.py:174
  37.2 21.5 %collective-permute-start.3 = (bf16[12,64,512]{2,1,0:T(8,128)(2,1)S(1)}, bf16[12,64,512]{2,1,0:T(8,128)(2,1)S(1)}, u32[]{:S(2)}, u32[]{:S(2)}) collective-permute-start(bf16[12,64,512]{2,1,0:T(8,128)(2,1)S(1)} %copy-done), channel_id=1, source_target_pairs={{0,1},{1,0},{2,3},{3,2},{4,5},{5,4},{6,7},{7,6},{8,9},{9,8},{10,11... | collective-permute-start | bytes 2359304 | tf_op jit(solution)/shard_map/ppermute | solution.py:178
  40.9 15.1 %copy-start.3 = (bf16[128,256]{1,0:T(8,128)(2,1)}, bf16[128,256]{1,0:T(8,128)(2,1)S(1)}, u32[]{:S(2)}) copy-start(bf16[128,256]{1,0:T(8,128)(2,1)S(1)} %multiply_convert_fusion.r_3_.r_8_) | copy-start | bytes 196612
  40.9 15.1 %collective-permute-start = (bf16[128,256]{1,0:T(8,128)(2,1)S(1)}, bf16[128,256]{1,0:T(8,128)(2,1)S(1)}, u32[]{:S(2)}, u32[]{:S(2)}) collective-permute-start(bf16[128,256]{1,0:T(8,128)(2,1)S(1)} %multiply_convert_fusion.r_3_.r_8_), channel_id=1, source_target_pairs={{0,24},{24,48},{48,72},{72,96},{96,120},{120,144},{144,168},{168,1... | collective-permute-start | bytes 196616 | tf_op jit(solution)/shard_map/ppermute | solution.py:170
  55.9 0.6 copy-start.4
  58.7 0.9 copy-start.2
  65.8 20.4 %all-to-all-start.3 = ((bf16[8,144,256]{2,1,0:T(8,128)(2,1)}), bf16[8,144,256]{2,1,0:T(8,128)(2,1)S(1)}, u32[]{:S(2)}, u32[]{:S(2)}) async-start(bf16[8,144,256]{2,1,0:T(8,128)(2,1)} %get-tuple-element.19), calls=%async_computation.3 | async-start | bytes 1179648 | tf_op jit(solution)/shard_map/all_to_all | solution.py:174
  76.8 5.1 %collective-permute-start.1 = (bf16[12,128,256]{2,1,0:T(8,128)(2,1)}, bf16[12,128,256]{2,1,0:T(8,128)(2,1)S(1)}, u32[]{:S(2)}, u32[]{:S(2)}) collective-permute-start(bf16[12,128,256]{2,1,0:T(8,128)(2,1)} %sent.1), channel_id=1, source_target_pairs={{0,1},{1,0},{2,3},{3,2},{4,5},{5,4},{6,7},{7,6},{8,9},{9,8},{10,11... | collective-permute-start | bytes 2359304 | tf_op jit(solution)/shard_map/ppermute | solution.py:178
  81.9 0.9 copy-start.1
  86.2 16.8 %all-to-all-start = ((bf16[12,128,256]{2,1,0:T(8,128)(2,1)}), bf16[12,128,256]{2,1,0:T(8,128)(2,1)S(1)}, u32[]{:S(2)}, u32[]{:S(2)}) async-start(bf16[12,128,256]{2,1,0:T(8,128)(2,1)} %kept.1), calls=%async_computation | async-start | bytes 1572864 | tf_op jit(solution)/shard_map/all_to_all | solution.py:174
  90.4 7.4 %collective-permute-start.5 = (bf16[8,64,768]{2,1,0:T(8,128)(2,1)S(1)}, bf16[8,64,768]{2,1,0:T(8,128)(2,1)S(1)}, u32[]{:S(2)}, u32[]{:S(2)}) collective-permute-start(bf16[8,64,768]{2,1,0:T(8,128)(2,1)S(1)} %all-to-all-done.2), channel_id=1, source_target_pairs={{0,1},{1,0},{2,3},{3,2},{4,5},{5,4},{6,7},{7,6},{8,9},{9,8},{10,11... | collective-permute-start | bytes 2359304 | tf_op jit(solution)/shard_map/ppermute | solution.py:178
  96.4 19.9 %copy-start.7 = (bf16[128,256]{1,0:T(8,128)(2,1)S(1)}, bf16[128,256]{1,0:T(8,128)(2,1)}, u32[]{:S(2)}) copy-start(bf16[128,256]{1,0:T(8,128)(2,1)} %get-tuple-element.16.r_2_) | copy-start | bytes 196612
  103.0 47.1 %all-to-all-start.4 = ((bf16[4,208,256]{2,1,0:T(8,128)(2,1)}), bf16[4,208,256]{2,1,0:T(8,128)(2,1)S(1)}, u32[]{:S(2)}, u32[]{:S(2)}) async-start(bf16[4,208,256]{2,1,0:T(8,128)(2,1)} %pad_maximum_fusion), calls=%async_computation.4 | async-start | bytes 851968 | tf_op jit(solution)/shard_map/all_to_all | solution.py:174
  116.3 31.1 %collective-permute-start.4 = (bf16[128,256]{1,0:T(8,128)(2,1)S(1)}, bf16[128,256]{1,0:T(8,128)(2,1)S(1)}, u32[]{:S(2)}, u32[]{:S(2)}) collective-permute-start(bf16[128,256]{1,0:T(8,128)(2,1)S(1)} %copy-done.7), channel_id=1, source_target_pairs={{24,0},{48,24},{72,48},{96,72},{120,96},{144,120},{168,144},{192,1... | collective-permute-start | bytes 196616 | tf_op jit(solution)/shard_map/ppermute | solution.py:170
  147.4 0.6 copy-start.8

commit v3 on v2

--- a/solution.py
+++ b/solution.py
@@ -7,6 +7,7 @@
 
 SEQ, CHAN, CHIPS = ("zh", "y"), ("zl", "x", "core"), ("zl", "x")
 F32, BF16 = jnp.float32, jnp.bfloat16
+TIED = ("pick",)
 SMEM = pl.BlockSpec(memory_space=pltpu.SMEM)
 VMEM = pl.BlockSpec(memory_space=pltpu.VMEM)
 
@@ -132,24 +133,31 @@
             out_ref[peer, :, tile * lanes : (tile + 1) * lanes] = jnp.where(low, half(a, False), half(b, True)).astype(BF16)
 
 
-def project_sent(docs, where_ref, gated_ref, w_ref, out_ref):
+def columns_to(docs, where_ref, n_zl, n_x, step, core, width):
+    zl = lax.rem(where_ref[docs + 2] + step // n_x, n_zl)
+    x = lax.rem(where_ref[docs + 3] + step % n_x, n_x)
+    return pl.ds(pl.multiple_of(((zl * n_x + x) * 2 + core) * width, width), width)
+
+
+def project_sent(docs, n_zl, n_x, where_ref, gated_ref, w_ref, out_ref):
     blocks, _, width = out_ref.shape
     core = 1 - where_ref[docs + 1]
-    for block in range(blocks):
-        lanes = pl.ds(pl.multiple_of((2 * block + core) * width, width), width)
-        out_ref[block] = jnp.dot(gated_ref[...], w_ref[:, lanes], preferred_element_type=F32).astype(BF16)
-
-
-def project_kept(docs, where_ref, gated_ref, w_ref, came_ref, out_ref):
-    blocks, _, width = out_ref.shape
+    for step in range(blocks):
+        lanes = columns_to(docs, where_ref, n_zl, n_x, step, core, width)
+        out_ref[step] = jnp.dot(gated_ref[...], w_ref[:, lanes], preferred_element_type=F32).astype(BF16)
+
+
+def project_kept(docs, n_zl, n_x, where_ref, gated_ref, w_ref, came_ref, *out_refs):
+    blocks, _, width = came_ref.shape
     core = where_ref[docs + 1]
-    for block in range(blocks):
-        lanes = pl.ds(pl.multiple_of((2 * block + core) * width, width), width)
+    for step in range(blocks):
+        lanes = columns_to(docs, where_ref, n_zl, n_x, step, core, width)
         total = jnp.dot(gated_ref[...], w_ref[:, lanes], preferred_element_type=F32)
-        out_ref[block] = (total + came_ref[block].astype(F32)).astype(BF16)
+        out_refs[step // n_x][step % n_x] = (total + came_ref[step].astype(F32)).astype(BF16)
 
 
 def call(kernel, outs, ins, scratch=(), name=None):
+    ins = [a if a.dtype == jnp.int32 or name not in TIED else pltpu.with_memory_space_constraint(a, pltpu.VMEM) for a in ins]
     return pl.pallas_call(
         kernel,
         out_shape=outs,
@@ -157,6 +165,7 @@
         out_specs=jax.tree.map(lambda _: VMEM, outs),
         scratch_shapes=list(scratch),
         name=name,
+        compiler_params=pltpu.CompilerParams(vmem_limit_bytes=16 << 20),
     )(*ins)
 
 
@@ -174,6 +183,11 @@
     return lax.all_to_all(value, axes, 0, 0, tiled=True)
 
 
+def turned(value, axis, steps):
+    count = lax.axis_size(axis)
+    return lax.ppermute(value, axis, [(source, (source + steps) % count) for source in range(count)])
+
+
 def swap_cores(value):
     return lax.ppermute(value, "core", [(0, 1), (1, 0)])
 
@@ -182,19 +196,15 @@
     rows, width = query_in.shape
     groups, length = filters.shape
     part, per_group, docs = rows // 2, width // groups, doc_lengths.shape[0]
-    n_zh, n_y, n_chip = lax.axis_size("zh"), lax.axis_size("y"), lax.axis_size(CHIPS)
+    n_zh, n_y, n_zl, n_x = (lax.axis_size(a) for a in ("zh", "y", "zl", "x"))
+    n_chip = n_zl * n_x
     core, place = lax.axis_index("core"), lax.axis_index(SEQ)
     columns = n_chip * 2 * width // (n_zh * n_y)
-    where = jnp.concatenate([doc_lengths, jnp.stack([place * rows, core]).astype(jnp.int32)])
-
-    halves = cotangent.reshape(2, part, width)
-    kept = lax.dynamic_index_in_dim(halves, core, 0, keepdims=False)
-    came = swap_cores(lax.dynamic_index_in_dim(halves, 1 - core, 0, keepdims=False))
-    both = jnp.where(core == 0, jnp.concatenate([kept, came], 1), jnp.concatenate([came, kept], 1))
-    mine = exchange(jnp.broadcast_to(both[None], (n_chip, part, 2 * width)), CHIPS)
-    picked = call(lambda *r: pick_kernel(64, columns, *r), like((n_y, part, n_zh * columns)), [mine], name="pick")
-    picked = exchange(picked, "y")
-    other = swap_cores(mine)
+    spots = jnp.stack([place * rows, core, lax.axis_index("zl"), lax.axis_index("x")])
+    where = jnp.concatenate([doc_lengths, spots.astype(jnp.int32)])
+
+    halves = jnp.broadcast_to(cotangent.reshape(1, 2, part, width), (n_chip, 2, part, width))
+    mine = exchange(halves.reshape(2 * n_chip, part, width), CHAN)
 
     product = (key_in.astype(F32) * value_in.astype(F32)).astype(BF16)
     prev = shifted(product, SEQ, 1)
@@ -206,26 +216,34 @@
         lambda *r: filter_kernel(docs, per_group, *r), (like((rows, width), F32), like((rows, width))),
         [where, ahead, prev, product, query_in], name="filter",
     )
+    sent = call(
+        lambda *r: project_sent(docs, n_zl, n_x, *r), like((n_chip, rows, width)), [where, gated, w_out], name="sent"
+    )
+    mine, sent = lax.optimization_barrier((mine, sent))
+    picked = call(lambda *r: pick_kernel(64, columns, *r), like((n_y, part, n_zh * columns)), [mine], name="pick")
+    picked = exchange(picked, "y")
+    other, came = swap_cores(mine), swap_cores(sent)
+    parts = call(
+        lambda *r: project_kept(docs, n_zl, n_x, *r), (like((n_x, rows, width)),) * n_zl,
+        [where, gated, w_out, came], name="kept",
+    )
     gate, grad_query, pay = call(
         lambda *r: grad_kernel(docs, per_group, *r),
         (like((rows, width)), like((rows, width)), like((n_y, rows + groups, width))),
         [where, mine, other, w_out, query_in, filtered, gated, prev, product],
         [pltpu.VMEM((rows, width), F32)], name="grad",
     )
+    pay, parts = lax.optimization_barrier((pay, parts))
     gathered = exchange(pay, "y")
     picked_other = swap_cores(picked)
-
-    sent = call(lambda *r: project_sent(docs, *r), like((n_chip, rows, width)), [where, gated, w_out], name="sent")
-    pair = call(
-        lambda *r: project_kept(docs, *r), like((n_chip, rows, width)), [where, gated, w_out, swap_cores(sent)], name="kept"
-    )
-    block_out = jnp.sum(exchange(pair, CHIPS).astype(F32), axis=0).astype(BF16)
-
     following = shifted(gate, SEQ, -1)
     grad_key, grad_value = call(
         lambda *r: back_kernel(docs, per_group, *r), (like((rows, width)), like((rows, width))),
         [where, behind, gate, following, key_in, value_in], name="back",
     )
+    along_z = sum((turned(parts[k], "zl", k).astype(F32) for k in range(1, n_zl)), parts[0].astype(F32)).astype(BF16)
+    gathered, grad_key, grad_value, along_z = lax.optimization_barrier((gathered, grad_key, grad_value, along_z))
+    block_out = sum((turned(along_z[k], "x", k).astype(F32) for k in range(1, n_x)), along_z[0].astype(F32)).astype(BF16)
 
     upper, lower = gathered[:, :part], gathered[:, part:rows]
     weight = jnp.einsum("ytn,ytc->nc", picked, jnp.where(core == 0, upper, lower), preferred_element_type=F32)

time: 152 us -> 131 us (0.86)
  the two profiles are of different devices: /device:TPU:121 before, /device:TPU:62 now
where the time goes in v3:
time: 131 us; the launch traced here: 130 us
  starting transfers between devices  73 us (56%)
  waiting for transfers between devices  25.4 us (19%)
  local copies, waits for them, and re-layouts  14.5 us (11%)
  Pallas kernels  10.8 us (8%)
  other arithmetic  3.54 us (3%)
  matrix products  1.97 us (2%)
    all_to_all x4, starting transfers between devices, exchange(): return lax.all_to_all(value, axes, 0, 0, tiled=True)  38.8 us
    ppermute x5, starting transfers between devices, turned(): lax.ppermute(value, axis, [(source, (source + steps) % count) for source...  16.2 us
    ppermute x2, waiting for transfers between devices, shifted(): lax.ppermute(value, axis, [(source, source + steps) for source in range(l...  13.4 us
    ppermute x2, starting transfers between devices, shifted(): lax.ppermute(value, axis, [(source, source + steps) for source in range(l...  11.7 us
    pallas_call x6, Pallas kernels, call(): pl.pallas_call(kernel, out_shape=outs, in_specs=[SMEM if a.dtype == jnp.i...  10.8 us
    unnamed x35, local copies, waits for them, and re-layouts  10.3 us
    all_to_all x4, waiting for transfers between devices, exchange(): return lax.all_to_all(value, axes, 0, 0, tiled=True)  9.54 us
    ppermute x3, starting transfers between devices, swap_cores(): return lax.ppermute(value, 'core', [(0, 1), (1, 0)])  6.37 us
  transfers between devices with their start and end apart: 14, of which 6 were waited for; matrix products, arithmetic and copies ran while one was open for 4% of the time, Pallas kernels for 7%

profile of v3, /device:TPU:62, one launch (start us, length us, event | category | flops | bytes accessed | tf_op | source)
XLA Modules:
  0.0 130.1 jit_solution(6838816141236711677)
XLA Ops:
  0.6 1.8 %broadcast_in_dim.7 = bf16[12,2,64,256]{3,2,1,0:T(8,128)(2,1)} broadcast(bf16[2,64,256]{2,1,0:T(8,128)(2,1)} %bitcast.30), dimensions={1,2,3} | broadcast | bytes 851968 | tf_op jit(solution)/shard_map/broadcast_in_dim | solution.py:206
  2.5 8.5 %all-to-all-start = ((bf16[24,64,256]{2,1,0:T(8,128)(2,1)}), bf16[24,64,256]{2,1,0:T(8,128)(2,1)}, u32[]{:S(2)}, u32[]{:S(2)}) async-start(bf16[24,64,256]{2,1,0:T(8,128)(2,1)} %bitcast.5), calls=%async_computation | async-start | bytes 1572864 | tf_op jit(solution)/shard_map/all_to_all | solution.py:183
  11.0 0.9 multiply_convert_fusion.r_3_.r_8_
  11.8 8.3 %collective-permute-start = (bf16[128,256]{1,0:T(8,128)(2,1)S(1)}, bf16[128,256]{1,0:T(8,128)(2,1)S(1)}, u32[]{:S(2)}, u32[]{:S(2)}) collective-permute-start(bf16[128,256]{1,0:T(8,128)(2,1)S(1)} %multiply_convert_fusion.r_3_.r_8_), channel_id=1, source_target_pairs={{0,24},{24,48},{48,72},{72,96},{96,120},{120,144},{144,168},{168,1... | collective-permute-start | bytes 196616 | tf_op jit(solution)/shard_map/ppermute | solution.py:179
  20.2 0.8 rev.8
  21.1 0.7 concatenate.12.r_0_
  21.8 2.4 %collective-permute-done.r_2_.r_7_ = bf16[128,256]{1,0:T(8,128)(2,1)S(1)} collective-permute-done((bf16[128,256]{1,0:T(8,128)(2,1)S(1)}, bf16[128,256]{1,0:T(8,128)(2,1)S(1)}, u32[]{:S(2)}, u32[]{:S(2)}) %collective-permute-start) | collective-permute-done | bytes 65568 | tf_op jit(solution)/shard_map/ppermute | solution.py:179
  24.2 0.8 copy-done.5
  25.1 1.1 filter.1
  26.2 0.6 copy-done.10
  26.8 1.9 %copy-done = bf16[256,6144]{1,0:T(8,128)(2,1)S(1)} copy-done((bf16[256,6144]{1,0:T(8,128)(2,1)S(1)}, bf16[256,6144]{1,0:T(8,128)(2,1)}, u32[]{:S(2)}) %copy-start) | copy-done | bytes 3145752
  28.7 0.9 sent.1
  29.7 0.9 copy-done.3
  30.5 1.4 %pick.1 = bf16[8,64,768]{2,1,0:T(8,128)(2,1)S(1)} custom-call(bf16[24,64,256]{2,1,0:T(8,128)(2,1)} %all-to-all-done.r_1_.r_0_), custom_call_target="tpu_custom_call" | custom-call | tf_op jit(solution)/shard_map/pick/pallas_call | solution.py:161
  32.0 0.9 copy-done.2
  32.9 4.6 %all-to-all-start.2 = ((bf16[8,64,768]{2,1,0:T(8,128)(2,1)}), bf16[8,64,768]{2,1,0:T(8,128)(2,1)}, u32[]{:S(2)}, u32[]{:S(2)}) async-start(bf16[8,64,768]{2,1,0:T(8,128)(2,1)} %copy-done.2), calls=%async_computation.2 | async-start | bytes 1572864 | tf_op jit(solution)/shard_map/all_to_all | solution.py:183
  37.6 2.0 %collective-permute-start.2 = (bf16[12,128,256]{2,1,0:T(8,128)(2,1)}, bf16[12,128,256]{2,1,0:T(8,128)(2,1)S(1)}, u32[]{:S(2)}, u32[]{:S(2)}) collective-permute-start(bf16[12,128,256]{2,1,0:T(8,128)(2,1)} %copy-done.3), channel_id=1, source_target_pairs={{0,1},{1,0},{2,3},{3,2},{4,5},{5,4},{6,7},{7,6},{8,9},{9,8},{10,11... | collective-permute-start | bytes 2359304 | tf_op jit(solution)/shard_map/ppermute | solution.py:192
  39.6 2.4 %collective-permute-start.1 = (bf16[24,64,256]{2,1,0:T(8,128)(2,1)}, bf16[24,64,256]{2,1,0:T(8,128)(2,1)S(1)}, u32[]{:S(2)}, u32[]{:S(2)}) collective-permute-start(bf16[24,64,256]{2,1,0:T(8,128)(2,1)} %all-to-all-done.r_1_.r_0_), channel_id=1, source_target_pairs={{0,1},{1,0},{2,3},{3,2},{4,5},{5,4},{6,7},{7,6},{8,9},{9,8},{10,11... | collective-permute-start | bytes 2359304 | tf_op jit(solution)/shard_map/ppermute | solution.py:192
  42.1 1.0 kept.1
  43.0 0.7 copy-done.9
  43.8 0.7 copy-done.14
  44.5 0.7 copy-done.15
  45.2 4.7 %grad.1 = (bf16[128,256]{1,0:T(8,128)(2,1)S(1)}, bf16[128,256]{1,0:T(8,128)(2,1)}, bf16[8,144,256]{2,1,0:T(8,128)(2,1)S(1)}) custom-call(s32[20]{0:T(128)S(1)} %concatenate.12.r_0_, bf16[24,64,256]{2,1,0:T(8,128)(2,1)} %all-to-all-done.r_1_.r_0_, bf16[24,64,256]{2,1,0:T(8,128)(2,1)S(1)} %collective-permute-done.1.r_2_, bf16[256,6144]{1,0:T(8,128)(2,1)S(1)} %copy-done.1, ...), custom_call_target="tpu_custom_call" | custom-call | tf_op jit(solution)/shard_map/grad/pallas_call | solution.py:161
  49.9 0.8 copy-done.4
  50.7 0.6 copy-done.12
  51.3 5.0 %all-to-all-done.2 = bf16[8,64,768]{2,1,0:T(8,128)(2,1)} async-done(((bf16[8,64,768]{2,1,0:T(8,128)(2,1)}), bf16[8,64,768]{2,1,0:T(8,128)(2,1)}, u32[]{:S(2)}, u32[]{:S(2)}) %all-to-all-start.2) | async-done | bytes 786464 | tf_op jit(solution)/shard_map/all_to_all | solution.py:183
  56.4 8.1 %all-to-all-start.1 = ((bf16[8,144,256]{2,1,0:T(8,128)(2,1)}), bf16[8,144,256]{2,1,0:T(8,128)(2,1)S(1)}, u32[]{:S(2)}, u32[]{:S(2)}) async-start(bf16[8,144,256]{2,1,0:T(8,128)(2,1)} %copy-done.4), calls=%async_computation.1 | async-start | bytes 1179648 | tf_op jit(solution)/shard_map/all_to_all | solution.py:183
  64.4 3.0 %collective-permute-start.5 = (bf16[4,128,256]{2,1,0:T(8,128)(2,1)}, bf16[4,128,256]{2,1,0:T(8,128)(2,1)S(1)}, u32[]{:S(2)}, u32[]{:S(2)}) collective-permute-start(bf16[4,128,256]{2,1,0:T(8,128)(2,1)} %copy-done.15), channel_id=1, source_target_pairs={{0,16},{8,0},{16,8},{1,17},{9,1},{17,9},{2,18},{10,2},{18,10},{3,1... | collective-permute-start | bytes 786440 | tf_op jit(solution)/shard_map/ppermute | solution.py:188
  67.4 3.6 %collective-permute-start.4 = (bf16[4,128,256]{2,1,0:T(8,128)(2,1)}, bf16[4,128,256]{2,1,0:T(8,128)(2,1)S(1)}, u32[]{:S(2)}, u32[]{:S(2)}) collective-permute-start(bf16[4,128,256]{2,1,0:T(8,128)(2,1)} %copy-done.14), channel_id=1, source_target_pairs={{0,8},{8,16},{16,0},{1,9},{9,17},{17,1},{2,10},{10,18},{18,2},{3,1... | collective-permute-start | bytes 786440 | tf_op jit(solution)/shard_map/ppermute | solution.py:188
  71.0 1.9 %collective-permute-start.9 = (bf16[8,64,768]{2,1,0:T(8,128)(2,1)}, bf16[8,64,768]{2,1,0:T(8,128)(2,1)S(1)}, u32[]{:S(2)}, u32[]{:S(2)}) collective-permute-start(bf16[8,64,768]{2,1,0:T(8,128)(2,1)} %all-to-all-done.2), channel_id=1, source_target_pairs={{0,1},{1,0},{2,3},{3,2},{4,5},{5,4},{6,7},{7,6},{8,9},{9,8},{10,11... | collective-permute-start | bytes 2359304 | tf_op jit(solution)/shard_map/ppermute | solution.py:192
  72.9 3.4 %collective-permute-start.3 = (bf16[128,256]{1,0:T(8,128)(2,1)}, bf16[128,256]{1,0:T(8,128)(2,1)S(1)}, u32[]{:S(2)}, u32[]{:S(2)}) collective-permute-start(bf16[128,256]{1,0:T(8,128)(2,1)} %copy-done.12), channel_id=1, source_target_pairs={{24,0},{48,24},{72,48},{96,72},{120,96},{144,120},{168,144},{192,1... | collective-permute-start | bytes 196616 | tf_op jit(solution)/shard_map/ppermute | solution.py:179
  76.3 11.0 %collective-permute-done.3.r_3_ = bf16[128,256]{1,0:T(8,128)(2,1)S(1)} collective-permute-done((bf16[128,256]{1,0:T(8,128)(2,1)}, bf16[128,256]{1,0:T(8,128)(2,1)S(1)}, u32[]{:S(2)}, u32[]{:S(2)}) %collective-permute-start.3) | collective-permute-done | bytes 65568 | tf_op jit(solution)/shard_map/ppermute | solution.py:179
  87.3 0.8 copy-done.13
  88.2 1.7 %back.1 = (bf16[128,256]{1,0:T(8,128)(2,1)}, bf16[128,256]{1,0:T(8,128)(2,1)}) custom-call(s32[20]{0:T(128)S(1)} %concatenate.12.r_0_, f32[16,256]{1,0:T(8,128)S(1)} %concatenate.14.r_1_, bf16[128,256]{1,0:T(8,128)(2,1)S(1)} %copy-done.13, bf16[128,256]{1,0:T(8,128)(2,1)S(1)} %collective-permute-done.3.r_3_, bf16[128,256]{1,0:T(8,128)(2,1)S(1)} %copy-done.8, ...), custom_call_target="tpu_custom_call" | custom-call | tf_op jit(solution)/shard_map/back/pallas_call | solution.py:161
  89.9 1.0 add_convert_fusion
  91.0 1.6 %convolution_bitcast_fusion.1 = f32[768,256]{1,0:T(8,128)S(1)} fusion(bf16[8,64,768]{2,1,0:T(8,128)(2,1)} %all-to-all-done.2, pred[]{:T(512)S(6)} %eq.4, bf16[8,144,256]{2,1,0:T(8,128)(2,1)S(1)} %all-to-all-done.1), kind=kOutput, calls=%fused_computation.1 | convolution fusion | flops 201457664 | bytes 2097153 | tf_op jit(solution)/shard_map/ytn,ytc->nc/dot_general | solution.py:249
  92.5 0.4 fusion.1
  93.0 0.8 pad_maximum_fusion
  93.8 17.6 %all-to-all-start.3 = ((bf16[4,208,256]{2,1,0:T(8,128)(2,1)}), bf16[4,208,256]{2,1,0:T(8,128)(2,1)S(1)}, u32[]{:S(2)}, u32[]{:S(2)}) async-start(bf16[4,208,256]{2,1,0:T(8,128)(2,1)} %pad_maximum_fusion), calls=%async_computation.3 | async-start | bytes 851968 | tf_op jit(solution)/shard_map/all_to_all | solution.py:183
  111.4 2.5 %collective-permute-start.8 = (bf16[128,256]{1,0:T(8,128)(2,1)S(1)}, bf16[128,256]{1,0:T(8,128)(2,1)S(1)}, u32[]{:S(2)}, u32[]{:S(2)}) collective-permute-start(bf16[128,256]{1,0:T(8,128)(2,1)S(1)} %get-tuple-element.59), channel_id=1, source_target_pairs={{0,6},{2,0},{4,2},{6,4},{1,7},{3,1},{5,3},{7,5},{8,14},{10,8},{12,... | collective-permute-start | bytes 196616 | tf_op jit(solution)/shard_map/ppermute | solution.py:188
  113.9 2.5 %collective-permute-start.7 = (bf16[128,256]{1,0:T(8,128)(2,1)S(1)}, bf16[128,256]{1,0:T(8,128)(2,1)S(1)}, u32[]{:S(2)}, u32[]{:S(2)}) collective-permute-start(bf16[128,256]{1,0:T(8,128)(2,1)S(1)} %get-tuple-element.60), channel_id=1, source_target_pairs={{0,4},{2,6},{4,0},{6,2},{1,5},{3,7},{5,1},{7,3},{8,12},{10,14},{12... | collective-permute-start | bytes 196616 | tf_op jit(solution)/shard_map/ppermute | solution.py:188
  116.4 4.5 %collective-permute-start.6 = (bf16[128,256]{1,0:T(8,128)(2,1)S(1)}, bf16[128,256]{1,0:T(8,128)(2,1)S(1)}, u32[]{:S(2)}, u32[]{:S(2)}) collective-permute-start(bf16[128,256]{1,0:T(8,128)(2,1)S(1)} %get-tuple-element.58), channel_id=1, source_target_pairs={{0,2},{2,4},{4,6},{6,0},{1,3},{3,5},{5,7},{7,1},{8,10},{10,12},{12... | collective-permute-start | bytes 196616 | tf_op jit(solution)/shard_map/ppermute | solution.py:188
  121.0 0.6 collective-permute-done.7
  121.6 1.9 %collective-permute-done.6 = bf16[128,256]{1,0:T(8,128)(2,1)S(1)} collective-permute-done((bf16[128,256]{1,0:T(8,128)(2,1)S(1)}, bf16[128,256]{1,0:T(8,128)(2,1)S(1)}, u32[]{:S(2)}, u32[]{:S(2)}) %collective-permute-start.6) | collective-permute-done | bytes 65568 | tf_op jit(solution)/shard_map/ppermute | solution.py:188
  123.4 0.7 fusion.12
  124.1 4.5 %all-to-all-done.3 = bf16[4,208,256]{2,1,0:T(8,128)(2,1)S(1)} async-done(((bf16[4,208,256]{2,1,0:T(8,128)(2,1)}), bf16[4,208,256]{2,1,0:T(8,128)(2,1)S(1)}, u32[]{:S(2)}, u32[]{:S(2)}) %all-to-all-start.3) | async-done | bytes 426016 | tf_op jit(solution)/shard_map/all_to_all | solution.py:183
  128.7 0.7 fusion.13
  129.5 0.7 copy.14
  (43 shorter events, 0.5 us)
Async XLA Ops:
  2.5 28.1 %all-to-all-start = ((bf16[24,64,256]{2,1,0:T(8,128)(2,1)}), bf16[24,64,256]{2,1,0:T(8,128)(2,1)}, u32[]{:S(2)}, u32[]{:S(2)}) async-start(bf16[24,64,256]{2,1,0:T(8,128)(2,1)} %bitcast.5), calls=%async_computation | async-start | bytes 1572864 | tf_op jit(solution)/shard_map/all_to_all | solution.py:183
  11.8 12.4 %collective-permute-start = (bf16[128,256]{1,0:T(8,128)(2,1)S(1)}, bf16[128,256]{1,0:T(8,128)(2,1)S(1)}, u32[]{:S(2)}, u32[]{:S(2)}) collective-permute-start(bf16[128,256]{1,0:T(8,128)(2,1)S(1)} %multiply_convert_fusion.r_3_.r_8_), channel_id=1, source_target_pairs={{0,24},{24,48},{48,72},{72,96},{96,120},{120,144},{144,168},{168,1... | collective-permute-start | bytes 196616 | tf_op jit(solution)/shard_map/ppermute | solution.py:179
  24.2 0.8 copy-start.5
  26.2 0.7 copy-start.10
  26.8 1.9 %copy-start = (bf16[256,6144]{1,0:T(8,128)(2,1)S(1)}, bf16[256,6144]{1,0:T(8,128)(2,1)}, u32[]{:S(2)}) copy-start(bf16[256,6144]{1,0:T(8,128)(2,1)} %r_2_.3) | copy-start | bytes 9437188
  28.7 13.3 %copy-start.1 = (bf16[256,6144]{1,0:T(8,128)(2,1)S(1)}, bf16[256,6144]{1,0:T(8,128)(2,1)}, u32[]{:S(2)}) copy-start(bf16[256,6144]{1,0:T(8,128)(2,1)} %r_2_.3) | copy-start | bytes 9437188
  29.7 0.9 copy-start.3
  32.0 0.9 copy-start.2
  32.9 12.3 %copy-start.6 = (bf16[128,256]{1,0:T(8,128)(2,1)S(1)}, bf16[128,256]{1,0:T(8,128)(2,1)}, u32[]{:S(2)}) copy-start(bf16[128,256]{1,0:T(8,128)(2,1)} %r_4_.4) | copy-start | bytes 196612
  32.9 23.4 %all-to-all-start.2 = ((bf16[8,64,768]{2,1,0:T(8,128)(2,1)}), bf16[8,64,768]{2,1,0:T(8,128)(2,1)}, u32[]{:S(2)}, u32[]{:S(2)}) async-start(bf16[8,64,768]{2,1,0:T(8,128)(2,1)} %copy-done.2), calls=%async_computation.2 | async-start | bytes 1572864 | tf_op jit(solution)/shard_map/all_to_all | solution.py:183
  37.6 7.6 %copy-start.11 = (f32[128,256]{1,0:T(8,128)S(1)}, f32[128,256]{1,0:T(8,128)}, u32[]{:S(2)}) copy-start(f32[128,256]{1,0:T(8,128)} %copy-done.10) | copy-start | bytes 393220
  37.6 4.5 %collective-permute-start.2 = (bf16[12,128,256]{2,1,0:T(8,128)(2,1)}, bf16[12,128,256]{2,1,0:T(8,128)(2,1)S(1)}, u32[]{:S(2)}, u32[]{:S(2)}) collective-permute-start(bf16[12,128,256]{2,1,0:T(8,128)(2,1)} %copy-done.3), channel_id=1, source_target_pairs={{0,1},{1,0},{2,3},{3,2},{4,5},{5,4},{6,7},{7,6},{8,9},{9,8},{10,11... | collective-permute-start | bytes 2359304 | tf_op jit(solution)/shard_map/ppermute | solution.py:192
  39.6 5.6 %collective-permute-start.1 = (bf16[24,64,256]{2,1,0:T(8,128)(2,1)}, bf16[24,64,256]{2,1,0:T(8,128)(2,1)S(1)}, u32[]{:S(2)}, u32[]{:S(2)}) collective-permute-start(bf16[24,64,256]{2,1,0:T(8,128)(2,1)} %all-to-all-done.r_1_.r_0_), channel_id=1, source_target_pairs={{0,1},{1,0},{2,3},{3,2},{4,5},{5,4},{6,7},{7,6},{8,9},{9,8},{10,11... | collective-permute-start | bytes 2359304 | tf_op jit(solution)/shard_map/ppermute | solution.py:192
  43.0 0.7 copy-start.9
  43.8 0.7 copy-start.14
  44.5 0.7 copy-start.15
  45.2 31.1 %copy-start.16 = (bf16[16,128]{1,0:T(8,128)(2,1)S(1)}, bf16[16,128]{1,0:T(8,128)(2,1)}, u32[]{:S(2)}) copy-start(bf16[16,128]{1,0:T(8,128)(2,1)} %param.10) | copy-start | bytes 12292
  45.2 42.1 %copy-start.7 = (bf16[128,256]{1,0:T(8,128)(2,1)S(1)}, bf16[128,256]{1,0:T(8,128)(2,1)}, u32[]{:S(2)}) copy-start(bf16[128,256]{1,0:T(8,128)(2,1)} %r_5_.1) | copy-start | bytes 196612
  45.2 42.1 %copy-start.8 = (bf16[128,256]{1,0:T(8,128)(2,1)S(1)}, bf16[128,256]{1,0:T(8,128)(2,1)}, u32[]{:S(2)}) copy-start(bf16[128,256]{1,0:T(8,128)(2,1)} %r_4_.5) | copy-start | bytes 196612
  49.9 0.8 copy-start.4
  50.7 0.6 copy-start.12
  56.4 34.6 %all-to-all-start.1 = ((bf16[8,144,256]{2,1,0:T(8,128)(2,1)}), bf16[8,144,256]{2,1,0:T(8,128)(2,1)S(1)}, u32[]{:S(2)}, u32[]{:S(2)}) async-start(bf16[8,144,256]{2,1,0:T(8,128)(2,1)} %copy-done.4), calls=%async_computation.1 | async-start | bytes 1179648 | tf_op jit(solution)/shard_map/all_to_all | solution.py:183
  64.4 25.5 %collective-permute-start.5 = (bf16[4,128,256]{2,1,0:T(8,128)(2,1)}, bf16[4,128,256]{2,1,0:T(8,128)(2,1)S(1)}, u32[]{:S(2)}, u32[]{:S(2)}) collective-permute-start(bf16[4,128,256]{2,1,0:T(8,128)(2,1)} %copy-done.15), channel_id=1, source_target_pairs={{0,16},{8,0},{16,8},{1,17},{9,1},{17,9},{2,18},{10,2},{18,10},{3,1... | collective-permute-start | bytes 786440 | tf_op jit(solution)/shard_map/ppermute | solution.py:188
  67.4 22.5 %collective-permute-start.4 = (bf16[4,128,256]{2,1,0:T(8,128)(2,1)}, bf16[4,128,256]{2,1,0:T(8,128)(2,1)S(1)}, u32[]{:S(2)}, u32[]{:S(2)}) collective-permute-start(bf16[4,128,256]{2,1,0:T(8,128)(2,1)} %copy-done.14), channel_id=1, source_target_pairs={{0,8},{8,16},{16,0},{1,9},{9,17},{17,1},{2,10},{10,18},{18,2},{3,1... | collective-permute-start | bytes 786440 | tf_op jit(solution)/shard_map/ppermute | solution.py:188
  71.0 21.5 %collective-permute-start.9 = (bf16[8,64,768]{2,1,0:T(8,128)(2,1)}, bf16[8,64,768]{2,1,0:T(8,128)(2,1)S(1)}, u32[]{:S(2)}, u32[]{:S(2)}) collective-permute-start(bf16[8,64,768]{2,1,0:T(8,128)(2,1)} %all-to-all-done.2), channel_id=1, source_target_pairs={{0,1},{1,0},{2,3},{3,2},{4,5},{5,4},{6,7},{7,6},{8,9},{9,8},{10,11... | collective-permute-start | bytes 2359304 | tf_op jit(solution)/shard_map/ppermute | solution.py:192
  72.9 14.4 %collective-permute-start.3 = (bf16[128,256]{1,0:T(8,128)(2,1)}, bf16[128,256]{1,0:T(8,128)(2,1)S(1)}, u32[]{:S(2)}, u32[]{:S(2)}) collective-permute-start(bf16[128,256]{1,0:T(8,128)(2,1)} %copy-done.12), channel_id=1, source_target_pairs={{24,0},{48,24},{72,48},{96,72},{120,96},{144,120},{168,144},{192,1... | collective-permute-start | bytes 196616 | tf_op jit(solution)/shard_map/ppermute | solution.py:179
  87.3 0.8 copy-start.13
  93.8 34.9 %all-to-all-start.3 = ((bf16[4,208,256]{2,1,0:T(8,128)(2,1)}), bf16[4,208,256]{2,1,0:T(8,128)(2,1)S(1)}, u32[]{:S(2)}, u32[]{:S(2)}) async-start(bf16[4,208,256]{2,1,0:T(8,128)(2,1)} %pad_maximum_fusion), calls=%async_computation.3 | async-start | bytes 851968 | tf_op jit(solution)/shard_map/all_to_all | solution.py:183
  111.4 9.6 %collective-permute-start.8 = (bf16[128,256]{1,0:T(8,128)(2,1)S(1)}, bf16[128,256]{1,0:T(8,128)(2,1)S(1)}, u32[]{:S(2)}, u32[]{:S(2)}) collective-permute-start(bf16[128,256]{1,0:T(8,128)(2,1)S(1)} %get-tuple-element.59), channel_id=1, source_target_pairs={{0,6},{2,0},{4,2},{6,4},{1,7},{3,1},{5,3},{7,5},{8,14},{10,8},{12,... | collective-permute-start | bytes 196616 | tf_op jit(solution)/shard_map/ppermute | solution.py:188
  113.9 7.7 %collective-permute-start.7 = (bf16[128,256]{1,0:T(8,128)(2,1)S(1)}, bf16[128,256]{1,0:T(8,128)(2,1)S(1)}, u32[]{:S(2)}, u32[]{:S(2)}) collective-permute-start(bf16[128,256]{1,0:T(8,128)(2,1)S(1)} %get-tuple-element.60), channel_id=1, source_target_pairs={{0,4},{2,6},{4,0},{6,2},{1,5},{3,7},{5,1},{7,3},{8,12},{10,14},{12... | collective-permute-start | bytes 196616 | tf_op jit(solution)/shard_map/ppermute | solution.py:188
  116.4 7.0 %collective-permute-start.6 = (bf16[128,256]{1,0:T(8,128)(2,1)S(1)}, bf16[128,256]{1,0:T(8,128)(2,1)S(1)}, u32[]{:S(2)}, u32[]{:S(2)}) collective-permute-start(bf16[128,256]{1,0:T(8,128)(2,1)S(1)} %get-tuple-element.58), channel_id=1, source_target_pairs={{0,2},{2,4},{4,6},{6,0},{1,3},{3,5},{5,7},{7,1},{8,10},{10,12},{12... | collective-permute-start | bytes 196616 | tf_op jit(solution)/shard_map/ppermute | solution.py:188

commit v4 on v3

--- a/solution.py
+++ b/solution.py
@@ -5,9 +5,10 @@
 from jax.experimental.pallas import tpu as pltpu
 from jax.sharding import Mesh, PartitionSpec as P
 
-SEQ, CHAN, CHIPS = ("zh", "y"), ("zl", "x", "core"), ("zl", "x")
+SEQ, CHAN = ("zh", "y"), ("zl", "x", "core")
 F32, BF16 = jnp.float32, jnp.bfloat16
 TIED = ("pick",)
+LIMITS = {"entry": None}
 SMEM = pl.BlockSpec(memory_space=pltpu.SMEM)
 VMEM = pl.BlockSpec(memory_space=pltpu.VMEM)
 
@@ -54,6 +55,13 @@
             total = jnp.where(member == group, value, total)
         outs.append(total)
     return outs
+
+
+def entry_kernel(cot_ref, k_ref, v_ref, fan_ref, prod_ref):
+    part = fan_ref.shape[1]
+    for peer in range(fan_ref.shape[0]):
+        fan_ref[peer] = cot_ref[peer % 2 * part : (peer % 2 + 1) * part, :]
+    prod_ref[...] = (k_ref[...].astype(F32) * v_ref[...].astype(F32)).astype(BF16)
 
 
 def filter_kernel(docs, per_group, where_ref, taps_ref, prev_ref, prod_ref, q_ref, filt_ref, gated_ref):
@@ -164,8 +172,7 @@
         in_specs=[SMEM if a.dtype == jnp.int32 else VMEM for a in ins],
         out_specs=jax.tree.map(lambda _: VMEM, outs),
         scratch_shapes=list(scratch),
-        name=name,
-        compiler_params=pltpu.CompilerParams(vmem_limit_bytes=16 << 20),
+        compiler_params=pltpu.CompilerParams(vmem_limit_bytes=LIMITS.get(name, 16 << 20)),
     )(*ins)
 
 
@@ -192,7 +199,7 @@
     return lax.ppermute(value, "core", [(0, 1), (1, 0)])
 
 
-def body(query_in, key_in, value_in, filters, doc_lengths, w_out, cotangent):
+def block(query_in, key_in, value_in, filters, doc_lengths, w_out, cotangent):
     rows, width = query_in.shape
     groups, length = filters.shape
     part, per_group, docs = rows // 2, width // groups, doc_lengths.shape[0]
@@ -203,10 +210,10 @@
     spots = jnp.stack([place * rows, core, lax.axis_index("zl"), lax.axis_index("x")])
     where = jnp.concatenate([doc_lengths, spots.astype(jnp.int32)])
 
-    halves = jnp.broadcast_to(cotangent.reshape(1, 2, part, width), (n_chip, 2, part, width))
-    mine = exchange(halves.reshape(2 * n_chip, part, width), CHAN)
-
-    product = (key_in.astype(F32) * value_in.astype(F32)).astype(BF16)
+    fan, product = call(
+        entry_kernel, (like((2 * n_chip, part, width)), like((rows, width))), [cotangent, key_in, value_in], name="entry"
+    )
+    mine = exchange(fan, CHAN)
     prev = shifted(product, SEQ, 1)
     taps = filters.astype(F32)
     zeros = jnp.zeros((groups, 2 * rows - length), F32)
@@ -219,7 +226,7 @@
     sent = call(
         lambda *r: project_sent(docs, n_zl, n_x, *r), like((n_chip, rows, width)), [where, gated, w_out], name="sent"
     )
-    mine, sent = lax.optimization_barrier((mine, sent))
+    mine, gated = lax.optimization_barrier((mine, gated))
     picked = call(lambda *r: pick_kernel(64, columns, *r), like((n_y, part, n_zh * columns)), [mine], name="pick")
     picked = exchange(picked, "y")
     other, came = swap_cores(mine), swap_cores(sent)
@@ -233,7 +240,6 @@
         [where, mine, other, w_out, query_in, filtered, gated, prev, product],
         [pltpu.VMEM((rows, width), F32)], name="grad",
     )
-    pay, parts = lax.optimization_barrier((pay, parts))
     gathered = exchange(pay, "y")
     picked_other = swap_cores(picked)
     following = shifted(gate, SEQ, -1)
@@ -261,7 +267,7 @@
 def build(fine):
     both, rows = P(SEQ, CHAN), P(CHAN, None)
     return jax.shard_map(
-        body,
+        block,
         mesh=fine,
         in_specs=(both, both, both, rows, P(), rows, both),
         out_specs=(both, both, both, both, P(CHAN, SEQ), P(CHAN, SEQ)),
@@ -270,4 +276,5 @@
 
 
 def solution(mesh):
-    return build(Mesh(mesh.devices.reshape(4, 8, 3, 4, 2), SEQ + CHAN))
+    fine = Mesh(mesh.devices.reshape(4, 8, 3, 4, 2), SEQ + CHAN)
+    return build(fine)

time: 131 us -> 133 us (1.015)
  the two profiles are of different devices: /device:TPU:62 before, /device:TPU:6 now
where the time goes in v4:
time: 133 us; the launch traced here: 131 us
  starting transfers between devices  64.6 us (49%)
  waiting for transfers between devices  35.8 us (27%)
  Pallas kernels  15 us (11%)
  local copies, waits for them, and re-layouts  7.81 us (6%)
  other arithmetic  3.48 us (3%)
  matrix products  3.15 us (2%)
    all_to_all x4, starting transfers between devices, exchange(): return lax.all_to_all(value, axes, 0, 0, tiled=True)  40.2 us
    all_to_all x4, waiting for transfers between devices, exchange(): return lax.all_to_all(value, axes, 0, 0, tiled=True)  26.2 us
    ppermute x5, starting transfers between devices, turned(): lax.ppermute(value, axis, [(source, (source + steps) % count) for source...  15.6 us
    pallas_call x7, Pallas kernels, call(): pl.pallas_call(kernel, out_shape=outs, in_specs=[SMEM if a.dtype == jnp.i...  15 us
    ppermute x5, waiting for transfers between devices, turned(): lax.ppermute(value, axis, [(source, (source + steps) % count) for source...  9.09 us
    ppermute x3, starting transfers between devices, swap_cores(): return lax.ppermute(value, 'core', [(0, 1), (1, 0)])  6.24 us
    unnamed x27, local copies, waits for them, and re-layouts  5.41 us
  transfers between devices with their start and end apart: 14, of which 7 were waited for; matrix products, arithmetic and copies ran while one was open for 5% of the time, Pallas kernels for 9%

profile of v4, /device:TPU:6, one launch (start us, length us, event | category | flops | bytes accessed | tf_op | source)
XLA Modules:
  0.0 130.8 jit_solution(15234398685294126064)
XLA Ops:
  0.6 2.0 %shard_map.118 = (bf16[24,64,256]{2,1,0:T(8,128)(2,1)}, bf16[128,256]{1,0:T(8,128)(2,1)}) custom-call(bf16[128,256]{1,0:T(8,128)(2,1)} %cot_ref.1, bf16[128,256]{1,0:T(8,128)(2,1)} %r_4_.5, bf16[128,256]{1,0:T(8,128)(2,1)} %r_5_.1), custom_call_target="tpu_custom_call" | custom-call | tf_op jit(solution)/shard_map/pallas_call | solution.py:169
  2.6 13.7 %all-to-all-start = ((bf16[24,64,256]{2,1,0:T(8,128)(2,1)}), bf16[24,64,256]{2,1,0:T(8,128)(2,1)}, u32[]{:S(2)}, u32[]{:S(2)}) async-start(bf16[24,64,256]{2,1,0:T(8,128)(2,1)} %get-tuple-element.24), calls=%async_computation | async-start | bytes 1572864 | tf_op jit(solution)/shard_map/all_to_all | solution.py:190
  16.4 1.3 collective-permute-start
  17.7 0.8 rev.8
  18.4 0.1 pad.5.clone
  18.5 0.1 maximum_maximum_fusion.r_1_
  18.6 0.7 concatenate.12.r_0_
  19.3 0.6 collective-permute-done.r_2_.r_7_
  19.9 0.8 copy-done.3
  20.7 0.8 copy-done.5
  21.6 1.1 shard_map.119
  22.6 8.6 %all-to-all-done.r_1_.r_0_ = bf16[24,64,256]{2,1,0:T(8,128)(2,1)} async-done(((bf16[24,64,256]{2,1,0:T(8,128)(2,1)}), bf16[24,64,256]{2,1,0:T(8,128)(2,1)}, u32[]{:S(2)}, u32[]{:S(2)}) %all-to-all-start) | async-done | bytes 786464 | tf_op jit(solution)/shard_map/all_to_all | solution.py:190
  31.2 1.4 %shard_map.124 = bf16[8,64,768]{2,1,0:T(8,128)(2,1)S(1)} custom-call(bf16[24,64,256]{2,1,0:T(8,128)(2,1)} %all-to-all-done.r_1_.r_0_), custom_call_target="tpu_custom_call" | custom-call | tf_op jit(solution)/shard_map/pallas_call | solution.py:169
  32.7 0.9 copy-done.1
  33.6 4.3 %all-to-all-start.2 = ((bf16[8,64,768]{2,1,0:T(8,128)(2,1)}), bf16[8,64,768]{2,1,0:T(8,128)(2,1)}, u32[]{:S(2)}, u32[]{:S(2)}) async-start(bf16[8,64,768]{2,1,0:T(8,128)(2,1)} %copy-done.1), calls=%async_computation.2 | async-start | bytes 1572864 | tf_op jit(solution)/shard_map/all_to_all | solution.py:190
  37.9 1.9 %collective-permute-start.1 = (bf16[24,64,256]{2,1,0:T(8,128)(2,1)}, bf16[24,64,256]{2,1,0:T(8,128)(2,1)S(1)}, u32[]{:S(2)}, u32[]{:S(2)}) collective-permute-start(bf16[24,64,256]{2,1,0:T(8,128)(2,1)} %all-to-all-done.r_1_.r_0_), channel_id=1, source_target_pairs={{0,1},{1,0},{2,3},{3,2},{4,5},{5,4},{6,7},{7,6},{8,9},{9,8},{10,11... | collective-permute-start | bytes 2359304 | tf_op jit(solution)/shard_map/ppermute | solution.py:199
  39.9 1.8 %shard_map.122 = bf16[12,128,256]{2,1,0:T(8,128)(2,1)} custom-call(s32[20]{0:T(128)S(1)} %concatenate.12.r_0_, bf16[128,256]{1,0:T(8,128)(2,1)S(1)} %get-tuple-element.29.r_6_.r_1_, bf16[256,6144]{1,0:T(8,128)(2,1)S(1)} %copy-done), custom_call_target="tpu_custom_call" | custom-call | tf_op jit(solution)/shard_map/pallas_call | solution.py:169
  41.7 2.4 %collective-permute-start.3 = (bf16[12,128,256]{2,1,0:T(8,128)(2,1)}, bf16[12,128,256]{2,1,0:T(8,128)(2,1)}, u32[]{:S(2)}, u32[]{:S(2)}) collective-permute-start(bf16[12,128,256]{2,1,0:T(8,128)(2,1)} %shard_map.122), channel_id=1, source_target_pairs={{0,1},{1,0},{2,3},{3,2},{4,5},{5,4},{6,7},{7,6},{8,9},{9,8},{10,11... | collective-permute-start | bytes 2359304 | tf_op jit(solution)/shard_map/ppermute | solution.py:199
  44.1 4.6 %shard_map.120 = (bf16[128,256]{1,0:T(8,128)(2,1)S(1)}, bf16[128,256]{1,0:T(8,128)(2,1)}, bf16[8,144,256]{2,1,0:T(8,128)(2,1)S(1)}) custom-call(s32[20]{0:T(128)S(1)} %concatenate.12.r_0_, bf16[24,64,256]{2,1,0:T(8,128)(2,1)} %all-to-all-done.r_1_.r_0_, bf16[24,64,256]{2,1,0:T(8,128)(2,1)S(1)} %collective-permute-done.1.r_2_, bf16[256,6144]{1,0:T(8,128)(2,1)S(1)} %copy-done, ...), custom_call_target="tpu_custom_call" | custom-call | tf_op jit(solution)/shard_map/pallas_call | solution.py:169
  48.8 0.8 copy-done.2
  49.6 0.6 copy-done.10
  50.2 11.1 %all-to-all-done.2 = bf16[8,64,768]{2,1,0:T(8,128)(2,1)} async-done(((bf16[8,64,768]{2,1,0:T(8,128)(2,1)}), bf16[8,64,768]{2,1,0:T(8,128)(2,1)}, u32[]{:S(2)}, u32[]{:S(2)}) %all-to-all-start.2) | async-done | bytes 786464 | tf_op jit(solution)/shard_map/all_to_all | solution.py:190
  61.3 4.3 %all-to-all-start.1 = ((bf16[8,144,256]{2,1,0:T(8,128)(2,1)}), bf16[8,144,256]{2,1,0:T(8,128)(2,1)}, u32[]{:S(2)}, u32[]{:S(2)}) async-start(bf16[8,144,256]{2,1,0:T(8,128)(2,1)} %copy-done.2), calls=%async_computation.1 | async-start | bytes 1179648 | tf_op jit(solution)/shard_map/all_to_all | solution.py:190
  65.7 2.3 %shard_map.123 = (bf16[4,128,256]{2,1,0:T(8,128)(2,1)S(1)}, bf16[4,128,256]{2,1,0:T(8,128)(2,1)}, bf16[4,128,256]{2,1,0:T(8,128)(2,1)}) custom-call(s32[20]{0:T(128)S(1)} %concatenate.12.r_0_, bf16[128,256]{1,0:T(8,128)(2,1)S(1)} %get-tuple-element.29.r_6_.r_1_, bf16[256,6144]{1,0:T(8,128)(2,1)S(1)} %copy-done, bf16[12,128,256]{2,1,0:T(8,128)(2,1)} %collective-permute-done.3.r_3_), custom_call_target="tpu_custom_call" | custom-call | tf_op jit(solution)/shard_map/pallas_call | solution.py:169
  68.0 0.7 copy-done.9
  68.7 2.2 %collective-permute-start.5 = (bf16[4,128,256]{2,1,0:T(8,128)(2,1)}, bf16[4,128,256]{2,1,0:T(8,128)(2,1)S(1)}, u32[]{:S(2)}, u32[]{:S(2)}) collective-permute-start(bf16[4,128,256]{2,1,0:T(8,128)(2,1)} %get-tuple-element.36), channel_id=1, source_target_pairs={{0,16},{8,0},{16,8},{1,17},{9,1},{17,9},{2,18},{10,2},{18,10},{3,1... | collective-permute-start | bytes 786440 | tf_op jit(solution)/shard_map/ppermute | solution.py:195
  70.8 3.6 %collective-permute-start.4 = (bf16[4,128,256]{2,1,0:T(8,128)(2,1)}, bf16[4,128,256]{2,1,0:T(8,128)(2,1)S(1)}, u32[]{:S(2)}, u32[]{:S(2)}) collective-permute-start(bf16[4,128,256]{2,1,0:T(8,128)(2,1)} %get-tuple-element.35), channel_id=1, source_target_pairs={{0,8},{8,16},{16,0},{1,9},{9,17},{17,1},{2,10},{10,18},{18,2},{3,1... | collective-permute-start | bytes 786440 | tf_op jit(solution)/shard_map/ppermute | solution.py:195
  74.5 1.9 %collective-permute-start.9 = (bf16[8,64,768]{2,1,0:T(8,128)(2,1)}, bf16[8,64,768]{2,1,0:T(8,128)(2,1)S(1)}, u32[]{:S(2)}, u32[]{:S(2)}) collective-permute-start(bf16[8,64,768]{2,1,0:T(8,128)(2,1)} %all-to-all-done.2), channel_id=1, source_target_pairs={{0,1},{1,0},{2,3},{3,2},{4,5},{5,4},{6,7},{7,6},{8,9},{9,8},{10,11... | collective-permute-start | bytes 2359304 | tf_op jit(solution)/shard_map/ppermute | solution.py:199
  76.5 1.3 collective-permute-start.2
  77.8 6.8 %collective-permute-done.5 = bf16[4,128,256]{2,1,0:T(8,128)(2,1)S(1)} collective-permute-done((bf16[4,128,256]{2,1,0:T(8,128)(2,1)}, bf16[4,128,256]{2,1,0:T(8,128)(2,1)S(1)}, u32[]{:S(2)}, u32[]{:S(2)}) %collective-permute-start.5) | collective-permute-done | bytes 262176 | tf_op jit(solution)/shard_map/ppermute | solution.py:195
  84.6 1.0 add_convert_fusion
  85.7 1.7 %shard_map.121 = (bf16[128,256]{1,0:T(8,128)(2,1)}, bf16[128,256]{1,0:T(8,128)(2,1)}) custom-call(s32[20]{0:T(128)S(1)} %concatenate.12.r_0_, f32[16,256]{1,0:T(8,128)S(1)} %concatenate.14.r_1_, bf16[128,256]{1,0:T(8,128)(2,1)S(1)} %copy-done.11, bf16[128,256]{1,0:T(8,128)(2,1)S(1)} %collective-permute-done.2.r_3_, bf16[128,256]{1,0:T(8,128)(2,1)S(1)} %copy-done.7, ...), custom_call_target="tpu_custom_call" | custom-call | tf_op jit(solution)/shard_map/pallas_call | solution.py:169
  87.4 0.9 slice_reduce_fusion
  88.2 1.7 %convolution_bitcast_fusion.1 = f32[768,256]{1,0:T(8,128)S(1)} fusion(bf16[8,64,768]{2,1,0:T(8,128)(2,1)} %all-to-all-done.2, pred[]{:T(512)S(6)} %eq.4, bf16[8,144,256]{2,1,0:T(8,128)(2,1)} %all-to-all-done.1), kind=kOutput, calls=%fused_computation.1 | convolution fusion | flops 201457664 | bytes 2097153 | tf_op jit(solution)/shard_map/ytn,ytc->nc/dot_general | solution.py:255
  90.0 1.5 %fusion.1 = bf16[768,256]{1,0:T(8,128)(2,1)S(1)} fusion(f32[768,256]{1,0:T(8,128)S(1)} %convolution_bitcast_fusion.1, bf16[8,64,768]{2,1,0:T(8,128)(2,1)S(1)} %collective-permute-done.9, pred[]{:T(512)S(6)} %eq.4, bf16[8,144,256]{2,1,0:T(8,128)(2,1)} %all-to-all-done.1), kind=kOutput, calls=%fused_computation.3 | convolution fusion | flops 201850880 | bytes 2490369 | tf_op jit(solution)/shard_map/ytn,ytc->nc/dot_general | solution.py:256
  91.4 0.8 pad_maximum_fusion
  92.2 17.8 %all-to-all-start.3 = ((bf16[4,208,256]{2,1,0:T(8,128)(2,1)}), bf16[4,208,256]{2,1,0:T(8,128)(2,1)S(1)}, u32[]{:S(2)}, u32[]{:S(2)}) async-start(bf16[4,208,256]{2,1,0:T(8,128)(2,1)} %pad_maximum_fusion), calls=%async_computation.3 | async-start | bytes 851968 | tf_op jit(solution)/shard_map/all_to_all | solution.py:190
  110.1 2.7 %collective-permute-start.8 = (bf16[128,256]{1,0:T(8,128)(2,1)S(1)}, bf16[128,256]{1,0:T(8,128)(2,1)S(1)}, u32[]{:S(2)}, u32[]{:S(2)}) collective-permute-start(bf16[128,256]{1,0:T(8,128)(2,1)S(1)} %get-tuple-element.55), channel_id=1, source_target_pairs={{0,6},{2,0},{4,2},{6,4},{1,7},{3,1},{5,3},{7,5},{8,14},{10,8},{12,... | collective-permute-start | bytes 196616 | tf_op jit(solution)/shard_map/ppermute | solution.py:195
  112.8 2.8 %collective-permute-start.7 = (bf16[128,256]{1,0:T(8,128)(2,1)S(1)}, bf16[128,256]{1,0:T(8,128)(2,1)S(1)}, u32[]{:S(2)}, u32[]{:S(2)}) collective-permute-start(bf16[128,256]{1,0:T(8,128)(2,1)S(1)} %get-tuple-element.56), channel_id=1, source_target_pairs={{0,4},{2,6},{4,0},{6,2},{1,5},{3,7},{5,1},{7,3},{8,12},{10,14},{12... | collective-permute-start | bytes 196616 | tf_op jit(solution)/shard_map/ppermute | solution.py:195
  115.6 4.3 %collective-permute-start.6 = (bf16[128,256]{1,0:T(8,128)(2,1)S(1)}, bf16[128,256]{1,0:T(8,128)(2,1)S(1)}, u32[]{:S(2)}, u32[]{:S(2)}) collective-permute-start(bf16[128,256]{1,0:T(8,128)(2,1)S(1)} %get-tuple-element.54), channel_id=1, source_target_pairs={{0,2},{2,4},{4,6},{6,0},{1,3},{3,5},{5,7},{7,1},{8,10},{10,12},{12... | collective-permute-start | bytes 196616 | tf_op jit(solution)/shard_map/ppermute | solution.py:195
  119.9 0.6 collective-permute-done.7
  120.4 1.7 %collective-permute-done.6 = bf16[128,256]{1,0:T(8,128)(2,1)S(1)} collective-permute-done((bf16[128,256]{1,0:T(8,128)(2,1)S(1)}, bf16[128,256]{1,0:T(8,128)(2,1)S(1)}, u32[]{:S(2)}, u32[]{:S(2)}) %collective-permute-start.6) | collective-permute-done | bytes 65568 | tf_op jit(solution)/shard_map/ppermute | solution.py:195
  122.1 0.7 fusion.12
  122.8 6.5 %all-to-all-done.3 = bf16[4,208,256]{2,1,0:T(8,128)(2,1)S(1)} async-done(((bf16[4,208,256]{2,1,0:T(8,128)(2,1)}), bf16[4,208,256]{2,1,0:T(8,128)(2,1)S(1)}, u32[]{:S(2)}, u32[]{:S(2)}) %all-to-all-start.3) | async-done | bytes 426016 | tf_op jit(solution)/shard_map/all_to_all | solution.py:190
  129.4 0.7 fusion.13
  130.0 0.1 constant_dynamic-slice_fusion
  130.1 0.1 rev.9
  130.2 0.7 copy.14
  (34 shorter events, 0.1 us)
Async XLA Ops:
  0.6 39.2 %copy-start = (bf16[256,6144]{1,0:T(8,128)(2,1)S(1)}, bf16[256,6144]{1,0:T(8,128)(2,1)}, u32[]{:S(2)}) copy-start(bf16[256,6144]{1,0:T(8,128)(2,1)} %r_2_.3) | copy-start | bytes 9437188
  2.6 28.6 %all-to-all-start = ((bf16[24,64,256]{2,1,0:T(8,128)(2,1)}), bf16[24,64,256]{2,1,0:T(8,128)(2,1)}, u32[]{:S(2)}, u32[]{:S(2)}) async-start(bf16[24,64,256]{2,1,0:T(8,128)(2,1)} %get-tuple-element.24), calls=%async_computation | async-start | bytes 1572864 | tf_op jit(solution)/shard_map/all_to_all | solution.py:190
  16.4 3.5 %collective-permute-start = (bf16[128,256]{1,0:T(8,128)(2,1)}, bf16[128,256]{1,0:T(8,128)(2,1)S(1)}, u32[]{:S(2)}, u32[]{:S(2)}) collective-permute-start(bf16[128,256]{1,0:T(8,128)(2,1)} %get-tuple-element.25.r_3_.r_8_), channel_id=1, source_target_pairs={{0,24},{24,48},{48,72},{72,96},{96,120},{120,144},{144,168},{168,1... | collective-permute-start | bytes 196616 | tf_op jit(solution)/shard_map/ppermute | solution.py:186
  19.9 0.8 copy-start.3
  20.7 0.8 copy-start.5
  32.7 0.9 copy-start.1
  33.6 10.5 %copy-start.4 = (bf16[128,256]{1,0:T(8,128)(2,1)S(1)}, bf16[128,256]{1,0:T(8,128)(2,1)}, u32[]{:S(2)}) copy-start(bf16[128,256]{1,0:T(8,128)(2,1)} %r_4_.4) | copy-start | bytes 196612
  33.6 10.5 %copy-start.6 = (bf16[128,256]{1,0:T(8,128)(2,1)S(1)}, bf16[128,256]{1,0:T(8,128)(2,1)}, u32[]{:S(2)}) copy-start(bf16[128,256]{1,0:T(8,128)(2,1)} %get-tuple-element.25.r_3_.r_8_) | copy-start | bytes 196612
  33.6 27.8 %all-to-all-start.2 = ((bf16[8,64,768]{2,1,0:T(8,128)(2,1)}), bf16[8,64,768]{2,1,0:T(8,128)(2,1)}, u32[]{:S(2)}, u32[]{:S(2)}) async-start(bf16[8,64,768]{2,1,0:T(8,128)(2,1)} %copy-done.1), calls=%async_computation.2 | async-start | bytes 1572864 | tf_op jit(solution)/shard_map/all_to_all | solution.py:190
  37.9 6.2 %collective-permute-start.1 = (bf16[24,64,256]{2,1,0:T(8,128)(2,1)}, bf16[24,64,256]{2,1,0:T(8,128)(2,1)S(1)}, u32[]{:S(2)}, u32[]{:S(2)}) collective-permute-start(bf16[24,64,256]{2,1,0:T(8,128)(2,1)} %all-to-all-done.r_1_.r_0_), channel_id=1, source_target_pairs={{0,1},{1,0},{2,3},{3,2},{4,5},{5,4},{6,7},{7,6},{8,9},{9,8},{10,11... | collective-permute-start | bytes 2359304 | tf_op jit(solution)/shard_map/ppermute | solution.py:199
  41.7 24.0 %collective-permute-start.3 = (bf16[12,128,256]{2,1,0:T(8,128)(2,1)}, bf16[12,128,256]{2,1,0:T(8,128)(2,1)}, u32[]{:S(2)}, u32[]{:S(2)}) collective-permute-start(bf16[12,128,256]{2,1,0:T(8,128)(2,1)} %shard_map.122), channel_id=1, source_target_pairs={{0,1},{1,0},{2,3},{3,2},{4,5},{5,4},{6,7},{7,6},{8,9},{9,8},{10,11... | collective-permute-start | bytes 2359304 | tf_op jit(solution)/shard_map/ppermute | solution.py:199
  48.8 0.8 copy-start.2
  49.6 0.6 copy-start.10
  50.2 26.2 %copy-start.12 = (bf16[16,128]{1,0:T(8,128)(2,1)S(1)}, bf16[16,128]{1,0:T(8,128)(2,1)}, u32[]{:S(2)}) copy-start(bf16[16,128]{1,0:T(8,128)(2,1)} %param.10) | copy-start | bytes 12292
  50.2 35.4 %copy-start.7 = (bf16[128,256]{1,0:T(8,128)(2,1)S(1)}, bf16[128,256]{1,0:T(8,128)(2,1)}, u32[]{:S(2)}) copy-start(bf16[128,256]{1,0:T(8,128)(2,1)} %r_4_.5) | copy-start | bytes 196612
  50.2 35.4 %copy-start.8 = (bf16[128,256]{1,0:T(8,128)(2,1)S(1)}, bf16[128,256]{1,0:T(8,128)(2,1)}, u32[]{:S(2)}) copy-start(bf16[128,256]{1,0:T(8,128)(2,1)} %r_5_.1) | copy-start | bytes 196612
  61.3 15.1 %copy-start.11 = (bf16[128,256]{1,0:T(8,128)(2,1)S(1)}, bf16[128,256]{1,0:T(8,128)(2,1)}, u32[]{:S(2)}) copy-start(bf16[128,256]{1,0:T(8,128)(2,1)} %copy-done.10) | copy-start | bytes 196612
  61.3 26.1 %all-to-all-start.1 = ((bf16[8,144,256]{2,1,0:T(8,128)(2,1)}), bf16[8,144,256]{2,1,0:T(8,128)(2,1)}, u32[]{:S(2)}, u32[]{:S(2)}) async-start(bf16[8,144,256]{2,1,0:T(8,128)(2,1)} %copy-done.2), calls=%async_computation.1 | async-start | bytes 1179648 | tf_op jit(solution)/shard_map/all_to_all | solution.py:190
  67.9 0.7 copy-start.9
  68.7 15.9 %collective-permute-start.5 = (bf16[4,128,256]{2,1,0:T(8,128)(2,1)}, bf16[4,128,256]{2,1,0:T(8,128)(2,1)S(1)}, u32[]{:S(2)}, u32[]{:S(2)}) collective-permute-start(bf16[4,128,256]{2,1,0:T(8,128)(2,1)} %get-tuple-element.36), channel_id=1, source_target_pairs={{0,16},{8,0},{16,8},{1,17},{9,1},{17,9},{2,18},{10,2},{18,10},{3,1... | collective-permute-start | bytes 786440 | tf_op jit(solution)/shard_map/ppermute | solution.py:195
  70.8 13.7 %collective-permute-start.4 = (bf16[4,128,256]{2,1,0:T(8,128)(2,1)}, bf16[4,128,256]{2,1,0:T(8,128)(2,1)S(1)}, u32[]{:S(2)}, u32[]{:S(2)}) collective-permute-start(bf16[4,128,256]{2,1,0:T(8,128)(2,1)} %get-tuple-element.35), channel_id=1, source_target_pairs={{0,8},{8,16},{16,0},{1,9},{9,17},{17,1},{2,10},{10,18},{18,2},{3,1... | collective-permute-start | bytes 786440 | tf_op jit(solution)/shard_map/ppermute | solution.py:195
  74.5 15.4 %collective-permute-start.9 = (bf16[8,64,768]{2,1,0:T(8,128)(2,1)}, bf16[8,64,768]{2,1,0:T(8,128)(2,1)S(1)}, u32[]{:S(2)}, u32[]{:S(2)}) collective-permute-start(bf16[8,64,768]{2,1,0:T(8,128)(2,1)} %all-to-all-done.2), channel_id=1, source_target_pairs={{0,1},{1,0},{2,3},{3,2},{4,5},{5,4},{6,7},{7,6},{8,9},{9,8},{10,11... | collective-permute-start | bytes 2359304 | tf_op jit(solution)/shard_map/ppermute | solution.py:199
  76.5 9.2 %collective-permute-start.2 = (bf16[128,256]{1,0:T(8,128)(2,1)S(1)}, bf16[128,256]{1,0:T(8,128)(2,1)S(1)}, u32[]{:S(2)}, u32[]{:S(2)}) collective-permute-start(bf16[128,256]{1,0:T(8,128)(2,1)S(1)} %copy-done.11), channel_id=1, source_target_pairs={{24,0},{48,24},{72,48},{96,72},{120,96},{144,120},{168,144},{192,1... | collective-permute-start | bytes 196616 | tf_op jit(solution)/shard_map/ppermute | solution.py:186
  92.2 37.1 %all-to-all-start.3 = ((bf16[4,208,256]{2,1,0:T(8,128)(2,1)}), bf16[4,208,256]{2,1,0:T(8,128)(2,1)S(1)}, u32[]{:S(2)}, u32[]{:S(2)}) async-start(bf16[4,208,256]{2,1,0:T(8,128)(2,1)} %pad_maximum_fusion), calls=%async_computation.3 | async-start | bytes 851968 | tf_op jit(solution)/shard_map/all_to_all | solution.py:190
  110.1 9.8 %collective-permute-start.8 = (bf16[128,256]{1,0:T(8,128)(2,1)S(1)}, bf16[128,256]{1,0:T(8,128)(2,1)S(1)}, u32[]{:S(2)}, u32[]{:S(2)}) collective-permute-start(bf16[128,256]{1,0:T(8,128)(2,1)S(1)} %get-tuple-element.55), channel_id=1, source_target_pairs={{0,6},{2,0},{4,2},{6,4},{1,7},{3,1},{5,3},{7,5},{8,14},{10,8},{12,... | collective-permute-start | bytes 196616 | tf_op jit(solution)/shard_map/ppermute | solution.py:195
  112.8 7.7 %collective-permute-start.7 = (bf16[128,256]{1,0:T(8,128)(2,1)S(1)}, bf16[128,256]{1,0:T(8,128)(2,1)S(1)}, u32[]{:S(2)}, u32[]{:S(2)}) collective-permute-start(bf16[128,256]{1,0:T(8,128)(2,1)S(1)} %get-tuple-element.56), channel_id=1, source_target_pairs={{0,4},{2,6},{4,0},{6,2},{1,5},{3,7},{5,1},{7,3},{8,12},{10,14},{12... | collective-permute-start | bytes 196616 | tf_op jit(solution)/shard_map/ppermute | solution.py:195
  115.6 6.6 %collective-permute-start.6 = (bf16[128,256]{1,0:T(8,128)(2,1)S(1)}, bf16[128,256]{1,0:T(8,128)(2,1)S(1)}, u32[]{:S(2)}, u32[]{:S(2)}) collective-permute-start(bf16[128,256]{1,0:T(8,128)(2,1)S(1)} %get-tuple-element.54), channel_id=1, source_target_pairs={{0,2},{2,4},{4,6},{6,0},{1,3},{3,5},{5,7},{7,1},{8,10},{10,12},{12... | collective-permute-start | bytes 196616 | tf_op jit(solution)/shard_map/ppermute | solution.py:195

commit v5 on v4

--- a/solution.py
+++ b/solution.py
@@ -161,7 +161,7 @@
     for step in range(blocks):
         lanes = columns_to(docs, where_ref, n_zl, n_x, step, core, width)
         total = jnp.dot(gated_ref[...], w_ref[:, lanes], preferred_element_type=F32)
-        out_refs[step // n_x][step % n_x] = (total + came_ref[step].astype(F32)).astype(BF16)
+        out_refs[step % n_x][step // n_x] = (total + came_ref[step].astype(F32)).astype(BF16)
 
 
 def call(kernel, outs, ins, scratch=(), name=None):
@@ -223,15 +223,15 @@
         lambda *r: filter_kernel(docs, per_group, *r), (like((rows, width), F32), like((rows, width))),
         [where, ahead, prev, product, query_in], name="filter",
     )
-    sent = call(
-        lambda *r: project_sent(docs, n_zl, n_x, *r), like((n_chip, rows, width)), [where, gated, w_out], name="sent"
-    )
     mine, gated = lax.optimization_barrier((mine, gated))
     picked = call(lambda *r: pick_kernel(64, columns, *r), like((n_y, part, n_zh * columns)), [mine], name="pick")
     picked = exchange(picked, "y")
+    sent = call(
+        lambda *r: project_sent(docs, n_zl, n_x, *r), like((n_chip, rows, width)), [where, gated, w_out], name="sent"
+    )
     other, came = swap_cores(mine), swap_cores(sent)
     parts = call(
-        lambda *r: project_kept(docs, n_zl, n_x, *r), (like((n_x, rows, width)),) * n_zl,
+        lambda *r: project_kept(docs, n_zl, n_x, *r), (like((n_zl, rows, width)),) * n_x,
         [where, gated, w_out, came], name="kept",
     )
     gate, grad_query, pay = call(
@@ -247,9 +247,9 @@
         lambda *r: back_kernel(docs, per_group, *r), (like((rows, width)), like((rows, width))),
         [where, behind, gate, following, key_in, value_in], name="back",
     )
-    along_z = sum((turned(parts[k], "zl", k).astype(F32) for k in range(1, n_zl)), parts[0].astype(F32)).astype(BF16)
-    gathered, grad_key, grad_value, along_z = lax.optimization_barrier((gathered, grad_key, grad_value, along_z))
-    block_out = sum((turned(along_z[k], "x", k).astype(F32) for k in range(1, n_x)), along_z[0].astype(F32)).astype(BF16)
+    along_x = sum((turned(parts[k], "x", k).astype(F32) for k in range(1, n_x)), parts[0].astype(F32)).astype(BF16)
+    gathered, grad_key, grad_value, along_x = lax.optimization_barrier((gathered, grad_key, grad_value, along_x))
+    block_out = sum((turned(along_x[k], "zl", k).astype(F32) for k in range(1, n_zl)), along_x[0].astype(F32)).astype(BF16)
 
     upper, lower = gathered[:, :part], gathered[:, part:rows]
     weight = jnp.einsum("ytn,ytc->nc", picked, jnp.where(core == 0, upper, lower), preferred_element_type=F32)

time: 133 us -> 133 us (level)
  the two profiles are of different devices: /device:TPU:6 before, /device:TPU:56 now
where the time goes in v5:
time: 133 us; the launch traced here: 132 us
  starting transfers between devices  72.8 us (55%)
  waiting for transfers between devices  30 us (23%)
  Pallas kernels  15.4 us (12%)
  local copies, waits for them, and re-layouts  6.46 us (5%)
  matrix products  3.38 us (3%)
  other arithmetic  2.55 us (2%)
    all_to_all x4, starting transfers between devices, exchange(): return lax.all_to_all(value, axes, 0, 0, tiled=True)  40 us
    pallas_call x7, Pallas kernels, call(): pl.pallas_call(kernel, out_shape=outs, in_specs=[SMEM if a.dtype == jnp.i...  15.4 us
    ppermute x5, starting transfers between devices, turned(): lax.ppermute(value, axis, [(source, (source + steps) % count) for source...  15 us
    ppermute x2, waiting for transfers between devices, shifted(): lax.ppermute(value, axis, [(source, source + steps) for source in range(l...  13.2 us
    ppermute x2, starting transfers between devices, shifted(): lax.ppermute(value, axis, [(source, source + steps) for source in range(l...  11.7 us
    ppermute x5, waiting for transfers between devices, turned(): lax.ppermute(value, axis, [(source, (source + steps) % count) for source...  9.4 us
    all_to_all x4, waiting for transfers between devices, exchange(): return lax.all_to_all(value, axes, 0, 0, tiled=True)  7.36 us
    ppermute x3, starting transfers between devices, swap_cores(): return lax.ppermute(value, 'core', [(0, 1), (1, 0)])  6.22 us
  transfers between devices with their start and end apart: 14, of which 6 were waited for; matrix products, arithmetic and copies ran while one was open for 4% of the time, Pallas kernels for 9%

profile of v5, /device:TPU:56, one launch (start us, length us, event | category | flops | bytes accessed | tf_op | source)
XLA Modules:
  0.0 131.5 jit_solution(614079841147162750)
XLA Ops:
  0.6 2.0 %shard_map.118 = (bf16[24,64,256]{2,1,0:T(8,128)(2,1)}, bf16[128,256]{1,0:T(8,128)(2,1)}) custom-call(bf16[128,256]{1,0:T(8,128)(2,1)} %cot_ref.1, bf16[128,256]{1,0:T(8,128)(2,1)} %r_4_.5, bf16[128,256]{1,0:T(8,128)(2,1)} %r_5_.1), custom_call_target="tpu_custom_call" | custom-call | tf_op jit(solution)/shard_map/pallas_call | solution.py:169
  2.6 8.3 %all-to-all-start = ((bf16[24,64,256]{2,1,0:T(8,128)(2,1)}), bf16[24,64,256]{2,1,0:T(8,128)(2,1)}, u32[]{:S(2)}, u32[]{:S(2)}) async-start(bf16[24,64,256]{2,1,0:T(8,128)(2,1)} %get-tuple-element.25), calls=%async_computation | async-start | bytes 1572864 | tf_op jit(solution)/shard_map/all_to_all | solution.py:190
  10.9 8.3 %collective-permute-start = (bf16[128,256]{1,0:T(8,128)(2,1)}, bf16[128,256]{1,0:T(8,128)(2,1)S(1)}, u32[]{:S(2)}, u32[]{:S(2)}) collective-permute-start(bf16[128,256]{1,0:T(8,128)(2,1)} %get-tuple-element.26.r_3_.r_8_), channel_id=1, source_target_pairs={{0,24},{24,48},{48,72},{72,96},{96,120},{120,144},{144,168},{168,1... | collective-permute-start | bytes 196616 | tf_op jit(solution)/shard_map/ppermute | solution.py:186
  19.2 0.8 rev.8
  20.0 0.1 pad.5.clone
  20.1 0.1 maximum_maximum_fusion.r_1_
  20.2 0.7 concatenate.12.r_0_
  20.9 3.6 %collective-permute-done.r_2_.r_7_ = bf16[128,256]{1,0:T(8,128)(2,1)S(1)} collective-permute-done((bf16[128,256]{1,0:T(8,128)(2,1)}, bf16[128,256]{1,0:T(8,128)(2,1)S(1)}, u32[]{:S(2)}, u32[]{:S(2)}) %collective-permute-start) | collective-permute-done | bytes 65568 | tf_op jit(solution)/shard_map/ppermute | solution.py:186
  24.4 0.8 copy-done.3
  25.3 0.8 copy-done.5
  26.1 1.1 shard_map.119
  27.2 0.0 all-to-all-done.r_1_.r_0_
  27.2 1.4 %shard_map.124 = bf16[8,64,768]{2,1,0:T(8,128)(2,1)S(1)} custom-call(bf16[24,64,256]{2,1,0:T(8,128)(2,1)} %all-to-all-done.r_1_.r_0_), custom_call_target="tpu_custom_call" | custom-call | tf_op jit(solution)/shard_map/pallas_call | solution.py:169
  28.7 0.9 copy-done.1
  29.6 9.1 %all-to-all-start.2 = ((bf16[8,64,768]{2,1,0:T(8,128)(2,1)}), bf16[8,64,768]{2,1,0:T(8,128)(2,1)}, u32[]{:S(2)}, u32[]{:S(2)}) async-start(bf16[8,64,768]{2,1,0:T(8,128)(2,1)} %copy-done.1), calls=%async_computation.2 | async-start | bytes 1572864 | tf_op jit(solution)/shard_map/all_to_all | solution.py:190
  38.6 1.9 %collective-permute-start.1 = (bf16[24,64,256]{2,1,0:T(8,128)(2,1)}, bf16[24,64,256]{2,1,0:T(8,128)(2,1)S(1)}, u32[]{:S(2)}, u32[]{:S(2)}) collective-permute-start(bf16[24,64,256]{2,1,0:T(8,128)(2,1)} %all-to-all-done.r_1_.r_0_), channel_id=1, source_target_pairs={{0,1},{1,0},{2,3},{3,2},{4,5},{5,4},{6,7},{7,6},{8,9},{9,8},{10,11... | collective-permute-start | bytes 2359304 | tf_op jit(solution)/shard_map/ppermute | solution.py:199
  40.5 1.8 %shard_map.122 = bf16[12,128,256]{2,1,0:T(8,128)(2,1)} custom-call(s32[20]{0:T(128)S(1)} %concatenate.12.r_0_, bf16[128,256]{1,0:T(8,128)(2,1)S(1)} %get-tuple-element.30.r_6_.r_1_, bf16[256,6144]{1,0:T(8,128)(2,1)S(1)} %copy-done), custom_call_target="tpu_custom_call" | custom-call | tf_op jit(solution)/shard_map/pallas_call | solution.py:169
  42.4 2.4 %collective-permute-start.3 = (bf16[12,128,256]{2,1,0:T(8,128)(2,1)}, bf16[12,128,256]{2,1,0:T(8,128)(2,1)}, u32[]{:S(2)}, u32[]{:S(2)}) collective-permute-start(bf16[12,128,256]{2,1,0:T(8,128)(2,1)} %shard_map.122), channel_id=1, source_target_pairs={{0,1},{1,0},{2,3},{3,2},{4,5},{5,4},{6,7},{7,6},{8,9},{9,8},{10,11... | collective-permute-start | bytes 2359304 | tf_op jit(solution)/shard_map/ppermute | solution.py:199
  44.8 4.6 %shard_map.120 = (bf16[128,256]{1,0:T(8,128)(2,1)}, bf16[128,256]{1,0:T(8,128)(2,1)}, bf16[8,144,256]{2,1,0:T(8,128)(2,1)S(1)}) custom-call(s32[20]{0:T(128)S(1)} %concatenate.12.r_0_, bf16[24,64,256]{2,1,0:T(8,128)(2,1)} %all-to-all-done.r_1_.r_0_, bf16[24,64,256]{2,1,0:T(8,128)(2,1)S(1)} %collective-permute-done.1.r_2_, bf16[256,6144]{1,0:T(8,128)(2,1)S(1)} %copy-done, ...), custom_call_target="tpu_custom_call" | custom-call | tf_op jit(solution)/shard_map/pallas_call | solution.py:169
  49.4 0.8 copy-done.2
  50.3 7.1 %all-to-all-done.2 = bf16[8,64,768]{2,1,0:T(8,128)(2,1)} async-done(((bf16[8,64,768]{2,1,0:T(8,128)(2,1)}), bf16[8,64,768]{2,1,0:T(8,128)(2,1)}, u32[]{:S(2)}, u32[]{:S(2)}) %all-to-all-start.2) | async-done | bytes 786464 | tf_op jit(solution)/shard_map/all_to_all | solution.py:190
  57.4 8.8 %all-to-all-start.1 = ((bf16[8,144,256]{2,1,0:T(8,128)(2,1)}), bf16[8,144,256]{2,1,0:T(8,128)(2,1)}, u32[]{:S(2)}, u32[]{:S(2)}) async-start(bf16[8,144,256]{2,1,0:T(8,128)(2,1)} %copy-done.2), calls=%async_computation.1 | async-start | bytes 1179648 | tf_op jit(solution)/shard_map/all_to_all | solution.py:190
  66.2 1.9 %collective-permute-start.9 = (bf16[8,64,768]{2,1,0:T(8,128)(2,1)}, bf16[8,64,768]{2,1,0:T(8,128)(2,1)}, u32[]{:S(2)}, u32[]{:S(2)}) collective-permute-start(bf16[8,64,768]{2,1,0:T(8,128)(2,1)} %all-to-all-done.2), channel_id=1, source_target_pairs={{0,1},{1,0},{2,3},{3,2},{4,5},{5,4},{6,7},{7,6},{8,9},{9,8},{10,11... | collective-permute-start | bytes 2359304 | tf_op jit(solution)/shard_map/ppermute | solution.py:199
  68.1 2.4 %shard_map.123 = (bf16[3,128,256]{2,1,0:T(8,128)(2,1)S(1)}, bf16[3,128,256]{2,1,0:T(8,128)(2,1)}, bf16[3,128,256]{2,1,0:T(8,128)(2,1)}, bf16[3,128,256]{2,1,0:T(8,128)(2,1)}) custom-call(s32[20]{0:T(128)S(1)} %concatenate.12.r_0_, bf16[128,256]{1,0:T(8,128)(2,1)S(1)} %get-tuple-element.30.r_6_.r_1_, bf16[256,6144]{1,0:T(8,128)(2,1)S(1)} %copy-done, ...), custom_call_target="tpu_custom_call" | custom-call | tf_op jit(solution)/shard_map/pallas_call | solution.py:169
  70.5 3.7 %collective-permute-start.6 = (bf16[3,128,256]{2,1,0:T(8,128)(2,1)}, bf16[3,128,256]{2,1,0:T(8,128)(2,1)S(1)}, u32[]{:S(2)}, u32[]{:S(2)}) collective-permute-start(bf16[3,128,256]{2,1,0:T(8,128)(2,1)} %get-tuple-element.38), channel_id=1, source_target_pairs={{0,6},{2,0},{4,2},{6,4},{1,7},{3,1},{5,3},{7,5},{8,14},{10,8},{12,... | collective-permute-start | bytes 589832 | tf_op jit(solution)/shard_map/ppermute | solution.py:195
  74.2 3.5 %collective-permute-start.5 = (bf16[3,128,256]{2,1,0:T(8,128)(2,1)}, bf16[3,128,256]{2,1,0:T(8,128)(2,1)S(1)}, u32[]{:S(2)}, u32[]{:S(2)}) collective-permute-start(bf16[3,128,256]{2,1,0:T(8,128)(2,1)} %get-tuple-element.37), channel_id=1, source_target_pairs={{0,4},{2,6},{4,0},{6,2},{1,5},{3,7},{5,1},{7,3},{8,12},{10,14},{12... | collective-permute-start | bytes 589832 | tf_op jit(solution)/shard_map/ppermute | solution.py:195
  77.7 1.9 %collective-permute-start.4 = (bf16[3,128,256]{2,1,0:T(8,128)(2,1)}, bf16[3,128,256]{2,1,0:T(8,128)(2,1)S(1)}, u32[]{:S(2)}, u32[]{:S(2)}) collective-permute-start(bf16[3,128,256]{2,1,0:T(8,128)(2,1)} %get-tuple-element.36), channel_id=1, source_target_pairs={{0,2},{2,4},{4,6},{6,0},{1,3},{3,5},{5,7},{7,1},{8,10},{10,12},{12... | collective-permute-start | bytes 589832 | tf_op jit(solution)/shard_map/ppermute | solution.py:195
  79.6 3.4 %collective-permute-start.2 = (bf16[128,256]{1,0:T(8,128)(2,1)}, bf16[128,256]{1,0:T(8,128)(2,1)S(1)}, u32[]{:S(2)}, u32[]{:S(2)}) collective-permute-start(bf16[128,256]{1,0:T(8,128)(2,1)} %get-tuple-element.32.r_2_), channel_id=1, source_target_pairs={{24,0},{48,24},{72,48},{96,72},{120,96},{144,120},{168,144},{192,1... | collective-permute-start | bytes 196616 | tf_op jit(solution)/shard_map/ppermute | solution.py:186
  83.0 9.7 %collective-permute-done.2.r_3_ = bf16[128,256]{1,0:T(8,128)(2,1)S(1)} collective-permute-done((bf16[128,256]{1,0:T(8,128)(2,1)}, bf16[128,256]{1,0:T(8,128)(2,1)S(1)}, u32[]{:S(2)}, u32[]{:S(2)}) %collective-permute-start.2) | collective-permute-done | bytes 65568 | tf_op jit(solution)/shard_map/ppermute | solution.py:186
  92.7 2.0 %shard_map.121 = (bf16[128,256]{1,0:T(8,128)(2,1)}, bf16[128,256]{1,0:T(8,128)(2,1)}) custom-call(s32[20]{0:T(128)S(1)} %concatenate.12.r_0_, f32[16,256]{1,0:T(8,128)S(1)} %concatenate.14.r_1_, bf16[128,256]{1,0:T(8,128)(2,1)} %get-tuple-element.32.r_2_, bf16[128,256]{1,0:T(8,128)(2,1)S(1)} %collective-permute-done.2.r_3_, bf16[128,256]{1,0:T(8,128)(2,1)S(1)} %copy-done.7, ...), custom_call_target="tpu_custom_call" | custom-call | tf_op jit(solution)/shard_map/pallas_call | solution.py:169
  94.8 0.1 add_convert_fusion
  94.9 0.0 all-to-all-done.1
  94.9 0.9 slice_reduce_fusion
  95.7 1.7 %convolution_bitcast_fusion.1 = f32[768,256]{1,0:T(8,128)S(1)} fusion(bf16[8,64,768]{2,1,0:T(8,128)(2,1)} %all-to-all-done.2, pred[]{:T(512)S(6)} %eq.4, bf16[8,144,256]{2,1,0:T(8,128)(2,1)} %all-to-all-done.1), kind=kOutput, calls=%fused_computation.1 | convolution fusion | flops 201457664 | bytes 2097153 | tf_op jit(solution)/shard_map/ytn,ytc->nc/dot_general | solution.py:255
  97.4 1.7 %fusion.1 = bf16[768,256]{1,0:T(8,128)(2,1)S(1)} fusion(f32[768,256]{1,0:T(8,128)S(1)} %convolution_bitcast_fusion.1, bf16[8,64,768]{2,1,0:T(8,128)(2,1)} %collective-permute-done.9, pred[]{:T(512)S(6)} %eq.4, bf16[8,144,256]{2,1,0:T(8,128)(2,1)} %all-to-all-done.1), kind=kOutput, calls=%fused_computation.3 | convolution fusion | flops 201850880 | bytes 2490369 | tf_op jit(solution)/shard_map/ytn,ytc->nc/dot_general | solution.py:256
  99.1 0.8 pad_maximum_fusion
  100.0 13.9 %all-to-all-start.3 = ((bf16[4,208,256]{2,1,0:T(8,128)(2,1)}), bf16[4,208,256]{2,1,0:T(8,128)(2,1)S(1)}, u32[]{:S(2)}, u32[]{:S(2)}) async-start(bf16[4,208,256]{2,1,0:T(8,128)(2,1)} %pad_maximum_fusion), calls=%async_computation.3 | async-start | bytes 851968 | tf_op jit(solution)/shard_map/all_to_all | solution.py:190
  113.8 1.9 %collective-permute-start.8 = (bf16[128,256]{1,0:T(8,128)(2,1)S(1)}, bf16[128,256]{1,0:T(8,128)(2,1)S(1)}, u32[]{:S(2)}, u32[]{:S(2)}) collective-permute-start(bf16[128,256]{1,0:T(8,128)(2,1)S(1)} %get-tuple-element.57), channel_id=1, source_target_pairs={{0,16},{8,0},{16,8},{1,17},{9,1},{17,9},{2,18},{10,2},{18,10},{3,1... | collective-permute-start | bytes 196616 | tf_op jit(solution)/shard_map/ppermute | solution.py:195
  115.8 3.9 %collective-permute-start.7 = (bf16[128,256]{1,0:T(8,128)(2,1)S(1)}, bf16[128,256]{1,0:T(8,128)(2,1)S(1)}, u32[]{:S(2)}, u32[]{:S(2)}) collective-permute-start(bf16[128,256]{1,0:T(8,128)(2,1)S(1)} %get-tuple-element.56), channel_id=1, source_target_pairs={{0,8},{8,16},{16,0},{1,9},{9,17},{17,1},{2,10},{10,18},{18,2},{3,1... | collective-permute-start | bytes 196616 | tf_op jit(solution)/shard_map/ppermute | solution.py:195
  119.7 6.9 %collective-permute-done.8 = bf16[128,256]{1,0:T(8,128)(2,1)S(1)} collective-permute-done((bf16[128,256]{1,0:T(8,128)(2,1)S(1)}, bf16[128,256]{1,0:T(8,128)(2,1)S(1)}, u32[]{:S(2)}, u32[]{:S(2)}) %collective-permute-start.8) | collective-permute-done | bytes 65568 | tf_op jit(solution)/shard_map/ppermute | solution.py:195
  126.6 2.5 %collective-permute-done.7 = bf16[128,256]{1,0:T(8,128)(2,1)S(1)} collective-permute-done((bf16[128,256]{1,0:T(8,128)(2,1)S(1)}, bf16[128,256]{1,0:T(8,128)(2,1)S(1)}, u32[]{:S(2)}, u32[]{:S(2)}) %collective-permute-start.7) | collective-permute-done | bytes 65568 | tf_op jit(solution)/shard_map/ppermute | solution.py:195
  129.1 0.7 fusion.11
  129.8 0.2 all-to-all-done.3
  130.0 0.1 convert_reduce_fusion
  130.1 0.7 fusion.12
  130.7 0.1 constant_dynamic-slice_fusion
  130.8 0.1 rev.9
  130.9 0.7 copy.14
  (28 shorter events, 0.1 us)
Async XLA Ops:
  0.6 39.9 %copy-start = (bf16[256,6144]{1,0:T(8,128)(2,1)S(1)}, bf16[256,6144]{1,0:T(8,128)(2,1)}, u32[]{:S(2)}) copy-start(bf16[256,6144]{1,0:T(8,128)(2,1)} %r_2_.3) | copy-start | bytes 9437188
  2.6 24.6 %all-to-all-start = ((bf16[24,64,256]{2,1,0:T(8,128)(2,1)}), bf16[24,64,256]{2,1,0:T(8,128)(2,1)}, u32[]{:S(2)}, u32[]{:S(2)}) async-start(bf16[24,64,256]{2,1,0:T(8,128)(2,1)} %get-tuple-element.25), calls=%async_computation | async-start | bytes 1572864 | tf_op jit(solution)/shard_map/all_to_all | solution.py:190
  10.9 13.5 %collective-permute-start = (bf16[128,256]{1,0:T(8,128)(2,1)}, bf16[128,256]{1,0:T(8,128)(2,1)S(1)}, u32[]{:S(2)}, u32[]{:S(2)}) collective-permute-start(bf16[128,256]{1,0:T(8,128)(2,1)} %get-tuple-element.26.r_3_.r_8_), channel_id=1, source_target_pairs={{0,24},{24,48},{48,72},{72,96},{96,120},{120,144},{144,168},{168,1... | collective-permute-start | bytes 196616 | tf_op jit(solution)/shard_map/ppermute | solution.py:186
  24.4 0.8 copy-start.3
  25.3 0.8 copy-start.5
  28.7 0.9 copy-start.1
  29.6 15.2 %copy-start.4 = (bf16[128,256]{1,0:T(8,128)(2,1)S(1)}, bf16[128,256]{1,0:T(8,128)(2,1)}, u32[]{:S(2)}) copy-start(bf16[128,256]{1,0:T(8,128)(2,1)} %r_4_.4) | copy-start | bytes 196612
  29.6 15.3 %copy-start.6 = (bf16[128,256]{1,0:T(8,128)(2,1)S(1)}, bf16[128,256]{1,0:T(8,128)(2,1)}, u32[]{:S(2)}) copy-start(bf16[128,256]{1,0:T(8,128)(2,1)} %get-tuple-element.26.r_3_.r_8_) | copy-start | bytes 196612
  29.6 27.8 %all-to-all-start.2 = ((bf16[8,64,768]{2,1,0:T(8,128)(2,1)}), bf16[8,64,768]{2,1,0:T(8,128)(2,1)}, u32[]{:S(2)}, u32[]{:S(2)}) async-start(bf16[8,64,768]{2,1,0:T(8,128)(2,1)} %copy-done.1), calls=%async_computation.2 | async-start | bytes 1572864 | tf_op jit(solution)/shard_map/all_to_all | solution.py:190
  38.6 6.2 %collective-permute-start.1 = (bf16[24,64,256]{2,1,0:T(8,128)(2,1)}, bf16[24,64,256]{2,1,0:T(8,128)(2,1)S(1)}, u32[]{:S(2)}, u32[]{:S(2)}) collective-permute-start(bf16[24,64,256]{2,1,0:T(8,128)(2,1)} %all-to-all-done.r_1_.r_0_), channel_id=1, source_target_pairs={{0,1},{1,0},{2,3},{3,2},{4,5},{5,4},{6,7},{7,6},{8,9},{9,8},{10,11... | collective-permute-start | bytes 2359304 | tf_op jit(solution)/shard_map/ppermute | solution.py:199
  42.4 25.7 %collective-permute-start.3 = (bf16[12,128,256]{2,1,0:T(8,128)(2,1)}, bf16[12,128,256]{2,1,0:T(8,128)(2,1)}, u32[]{:S(2)}, u32[]{:S(2)}) collective-permute-start(bf16[12,128,256]{2,1,0:T(8,128)(2,1)} %shard_map.122), channel_id=1, source_target_pairs={{0,1},{1,0},{2,3},{3,2},{4,5},{5,4},{6,7},{7,6},{8,9},{9,8},{10,11... | collective-permute-start | bytes 2359304 | tf_op jit(solution)/shard_map/ppermute | solution.py:199
  49.4 0.8 copy-start.2
  50.3 32.7 %copy-start.9 = (bf16[16,128]{1,0:T(8,128)(2,1)S(1)}, bf16[16,128]{1,0:T(8,128)(2,1)}, u32[]{:S(2)}) copy-start(bf16[16,128]{1,0:T(8,128)(2,1)} %param.10) | copy-start | bytes 12292
  50.3 42.5 %copy-start.7 = (bf16[128,256]{1,0:T(8,128)(2,1)S(1)}, bf16[128,256]{1,0:T(8,128)(2,1)}, u32[]{:S(2)}) copy-start(bf16[128,256]{1,0:T(8,128)(2,1)} %r_4_.5) | copy-start | bytes 196612
  50.3 42.5 %copy-start.8 = (bf16[128,256]{1,0:T(8,128)(2,1)S(1)}, bf16[128,256]{1,0:T(8,128)(2,1)}, u32[]{:S(2)}) copy-start(bf16[128,256]{1,0:T(8,128)(2,1)} %r_5_.1) | copy-start | bytes 196612
  57.4 37.5 %all-to-all-start.1 = ((bf16[8,144,256]{2,1,0:T(8,128)(2,1)}), bf16[8,144,256]{2,1,0:T(8,128)(2,1)}, u32[]{:S(2)}, u32[]{:S(2)}) async-start(bf16[8,144,256]{2,1,0:T(8,128)(2,1)} %copy-done.2), calls=%async_computation.1 | async-start | bytes 1179648 | tf_op jit(solution)/shard_map/all_to_all | solution.py:190
  66.2 31.2 %collective-permute-start.9 = (bf16[8,64,768]{2,1,0:T(8,128)(2,1)}, bf16[8,64,768]{2,1,0:T(8,128)(2,1)}, u32[]{:S(2)}, u32[]{:S(2)}) collective-permute-start(bf16[8,64,768]{2,1,0:T(8,128)(2,1)} %all-to-all-done.2), channel_id=1, source_target_pairs={{0,1},{1,0},{2,3},{3,2},{4,5},{5,4},{6,7},{7,6},{8,9},{9,8},{10,11... | collective-permute-start | bytes 2359304 | tf_op jit(solution)/shard_map/ppermute | solution.py:199
  70.5 24.2 %collective-permute-start.6 = (bf16[3,128,256]{2,1,0:T(8,128)(2,1)}, bf16[3,128,256]{2,1,0:T(8,128)(2,1)S(1)}, u32[]{:S(2)}, u32[]{:S(2)}) collective-permute-start(bf16[3,128,256]{2,1,0:T(8,128)(2,1)} %get-tuple-element.38), channel_id=1, source_target_pairs={{0,6},{2,0},{4,2},{6,4},{1,7},{3,1},{5,3},{7,5},{8,14},{10,8},{12,... | collective-permute-start | bytes 589832 | tf_op jit(solution)/shard_map/ppermute | solution.py:195
  74.2 20.6 %collective-permute-start.5 = (bf16[3,128,256]{2,1,0:T(8,128)(2,1)}, bf16[3,128,256]{2,1,0:T(8,128)(2,1)S(1)}, u32[]{:S(2)}, u32[]{:S(2)}) collective-permute-start(bf16[3,128,256]{2,1,0:T(8,128)(2,1)} %get-tuple-element.37), channel_id=1, source_target_pairs={{0,4},{2,6},{4,0},{6,2},{1,5},{3,7},{5,1},{7,3},{8,12},{10,14},{12... | collective-permute-start | bytes 589832 | tf_op jit(solution)/shard_map/ppermute | solution.py:195
  77.7 17.0 %collective-permute-start.4 = (bf16[3,128,256]{2,1,0:T(8,128)(2,1)}, bf16[3,128,256]{2,1,0:T(8,128)(2,1)S(1)}, u32[]{:S(2)}, u32[]{:S(2)}) collective-permute-start(bf16[3,128,256]{2,1,0:T(8,128)(2,1)} %get-tuple-element.36), channel_id=1, source_target_pairs={{0,2},{2,4},{4,6},{6,0},{1,3},{3,5},{5,7},{7,1},{8,10},{10,12},{12... | collective-permute-start | bytes 589832 | tf_op jit(solution)/shard_map/ppermute | solution.py:195
  79.6 13.1 %collective-permute-start.2 = (bf16[128,256]{1,0:T(8,128)(2,1)}, bf16[128,256]{1,0:T(8,128)(2,1)S(1)}, u32[]{:S(2)}, u32[]{:S(2)}) collective-permute-start(bf16[128,256]{1,0:T(8,128)(2,1)} %get-tuple-element.32.r_2_), channel_id=1, source_target_pairs={{24,0},{48,24},{72,48},{96,72},{120,96},{144,120},{168,144},{192,1... | collective-permute-start | bytes 196616 | tf_op jit(solution)/shard_map/ppermute | solution.py:186
  100.0 30.0 %all-to-all-start.3 = ((bf16[4,208,256]{2,1,0:T(8,128)(2,1)}), bf16[4,208,256]{2,1,0:T(8,128)(2,1)S(1)}, u32[]{:S(2)}, u32[]{:S(2)}) async-start(bf16[4,208,256]{2,1,0:T(8,128)(2,1)} %pad_maximum_fusion), calls=%async_computation.3 | async-start | bytes 851968 | tf_op jit(solution)/shard_map/all_to_all | solution.py:190
  113.8 12.7 %collective-permute-start.8 = (bf16[128,256]{1,0:T(8,128)(2,1)S(1)}, bf16[128,256]{1,0:T(8,128)(2,1)S(1)}, u32[]{:S(2)}, u32[]{:S(2)}) collective-permute-start(bf16[128,256]{1,0:T(8,128)(2,1)S(1)} %get-tuple-element.57), channel_id=1, source_target_pairs={{0,16},{8,0},{16,8},{1,17},{9,1},{17,9},{2,18},{10,2},{18,10},{3,1... | collective-permute-start | bytes 196616 | tf_op jit(solution)/shard_map/ppermute | solution.py:195
  115.8 13.3 %collective-permute-start.7 = (bf16[128,256]{1,0:T(8,128)(2,1)S(1)}, bf16[128,256]{1,0:T(8,128)(2,1)S(1)}, u32[]{:S(2)}, u32[]{:S(2)}) collective-permute-start(bf16[128,256]{1,0:T(8,128)(2,1)S(1)} %get-tuple-element.56), channel_id=1, source_target_pairs={{0,8},{8,16},{16,0},{1,9},{9,17},{17,1},{2,10},{10,18},{18,2},{3,1... | collective-permute-start | bytes 196616 | tf_op jit(solution)/shard_map/ppermute | solution.py:195
